TPU v7x, 256 devices: a whole 4x4x8 slice. The times are simulated.
256 devices in a mesh: tm: 4 (over y), space: 64 (over x, z, core).
Axes of the slice: x: 4, y: 4, z: 8, core: 2. Of those that a mesh axis runs over, the one named last changes fastest.
Arguments:
- anomalies: bfloat16 [16, 128, 262144], P('tm', None, 'space'), may hold values from -51 to 51
- obs_index: int32 [16, 65536], P('tm', 'space'), may hold values from 0 to 4095
- obs_weight: float32 [16, 65536], P('tm', 'space'), may hold values from 0.01 to 0.12
Outputs:
- smoothed: bfloat16 [16, 128, 262144], P('tm', None, 'space')
All inputs are finite; a program needn't handle non-finite values.
Results may differ from a plain program's by a relative error of at most 0.0034.
Values sent between devices are 32-bit elements; how exact they have to be, the bound alone decides.
No kernel may reach another device: no remote copies, remote signals or barrier semaphores. Data moves between devices by JAX's collectives and lax.ppermute only.
A program may use at most 64 MiB of HBM per device.

v0:
```python
import jax
import jax.numpy as jnp
from jax import lax
from jax.sharding import PartitionSpec as P


def in_blocks(shard, dim, size):
    before, after = (shard.shape[:dim], shard.shape[dim + 1 :])
    return jnp.moveaxis(shard.reshape(*before, size, -1, *after), dim, 0)


def summed_on_arrival(shard, axis, dim):
    size = lax.axis_size(axis)
    blocks = lax.all_to_all(in_blocks(shard, dim, size), axis, 0, 0, tiled=True)
    return jnp.sum(blocks, axis=0)


def filled_up(lines, size):
    spare = -lines.shape[0] % size
    if not spare:
        return lines
    return jnp.concatenate([lines, jnp.zeros((spare, *lines.shape[1:]), lines.dtype)])


def joined_along(blocks, dim):
    lengths = list(blocks.shape[1:])
    lengths[dim] *= blocks.shape[0]
    return jnp.moveaxis(blocks, 0, dim).reshape(lengths)


def copy_for_each(shard, axis):
    size = lax.axis_size(axis)
    return lax.all_to_all(
        jnp.broadcast_to(shard[None], (size, *shard.shape)), axis, 0, 0, tiled=True
    )


def gathered_copies(shard, axis, dim):
    return joined_along(copy_for_each(shard, axis), dim)


def nested_sum(shard, axes):
    lines = shard.reshape(-1, shard.shape[-1])
    own = summed_on_arrival(filled_up(lines, lax.axis_size(axes)), axes, 0)
    whole = gathered_copies(own, axes, 0)
    return whole[: len(lines)].reshape(shard.shape)


def folded_in_pairs(pieces, combine):
    while len(jax.tree.leaves(pieces)[0]) > 1:
        pieces = jax.vmap(combine)(*(pieces[side::2] for side in (0, 1)))
    return pieces[0]


def carried_in(shard, axis, combine, identity):
    size, index = (lax.axis_size(axis), lax.axis_index(axis))
    passed = jnp.arange(size) > index

    def kept(part, zero, own):
        part = jnp.where(
            passed.reshape(-1, *(1 for _ in own.shape)), part, jnp.asarray(zero, own.dtype)
        )
        return part[::-1]

    pieces = copy_for_each(shard, axis)
    return folded_in_pairs(kept(pieces, identity, shard), combine)


def transform(gram_total, spread_dof, identity):
    factor = jnp.linalg.cholesky(spread_dof * identity + gram_total)
    inverse_low = lax.linalg.triangular_solve(
        factor, jnp.broadcast_to(identity, gram_total.shape), left_side=True, lower=True
    )
    return spread_dof * jnp.einsum(
        "tkm,tkn->tmn", inverse_low, inverse_low, precision=lax.Precision.HIGHEST
    )


def advance(running, weight_now):
    return (jnp.dot(weight_now, running, precision=lax.Precision.HIGHEST), running)


def pick_cells(anomalies, obs_index):
    grid_cells = anomalies.shape[2]
    cell_ids = lax.broadcasted_iota(jnp.int32, (1, 1, grid_cells), 2)
    selector = (obs_index[:, :, None] == cell_ids).astype(jnp.bfloat16)
    return jnp.einsum("tmc,toc->tmo", anomalies, selector, preferred_element_type=jnp.float32)


def per_device(anomalies, obs_index, obs_weight):
    local_times, member_count, grid_cells = anomalies.shape
    spread_dof = float(member_count - 1)
    identity = jnp.eye(member_count, dtype=jnp.float32)
    picked = pick_cells(anomalies, obs_index)
    scaled = (picked * obs_weight[:, None, :]).astype(jnp.bfloat16)
    gram_part = jnp.einsum("tmo,tno->tmn", scaled, scaled, preferred_element_type=jnp.float32)
    summed = nested_sum(gram_part, "space")
    weights = transform(summed, spread_dof, identity)
    own_product = identity
    for position in range(local_times):
        own_product = jnp.dot(own_product, weights[position], precision=lax.Precision.HIGHEST)

    def compose(earlier, later_one):
        return jnp.dot(later_one, earlier, precision=lax.Precision.HIGHEST)

    suffix = carried_in(own_product, "tm", compose, identity)
    _, chains = lax.scan(advance, suffix, weights, reverse=True)
    chains_low = chains.astype(jnp.bfloat16)
    smoothed = jnp.einsum("tmn,tmc->tnc", chains_low, anomalies, preferred_element_type=jnp.float32)
    return smoothed.astype(jnp.bfloat16)


def solution(mesh):
    return jax.shard_map(
        per_device,
        mesh=mesh,
        in_specs=(P("tm", None, "space"), P("tm", "space"), P("tm", "space")),
        out_specs=P("tm", None, "space"),
        check_vma=False,
    )
```

profile of v0, /device:TPU:1, one launch (start us, length us, event | category | flops | bytes accessed | tf_op | source)
XLA Modules:
  0.0 176.1 jit_solution(5727485205409942545)
XLA Ops:
  0.0 25.9 %fusion.6 = f32[4,128,128]{2,1,0:T(8,128)S(1)} fusion(bf16[4,128,4096]{2,1,0:T(8,128)(2,1)} %param.5, s32[4,1024]{1,0:T(4,128)} %param.6, f32[4,1024]{1,0:T(4,128)} %param.7), kind=kOutput, calls=%fused_computation.11 | convolution fusion | flops 4447010816 | bytes 4489216 | tf_op jit(solution)/shard_map/tmo,tno->tmn/dot_general | solution.py:96
  25.9 24.7 %all_to_all.15 = f32[64,8,128]{2,1,0:T(8,128)S(1)} all-to-all(f32[64,8,128]{2,1,0:T(8,128)S(1)} %bitcast.51), channel_id=1, replica_groups=mesh['tm'=4,'space'=64] {'space'}, dimensions={0} | all-to-all | bytes 524288 | tf_op jit(solution)/shard_map/all_to_all | solution.py:14
  50.6 0.1 reduce_sum.9
  50.7 0.7 broadcast_in_dim.46
  51.4 6.0 %all-to-all-start.1 = ((f32[64,8,128]{2,1,0:T(8,128)}), f32[64,8,128]{2,1,0:T(8,128)S(1)}, u32[]{:S(2)}, u32[]{:S(2)}) async-start(f32[64,8,128]{2,1,0:T(8,128)} %broadcast_in_dim.46), calls=%async_computation.1 | async-start | bytes 524288 | tf_op jit(solution)/shard_map/all_to_all | solution.py:33
  57.5 0.1 copy.15
  57.6 11.8 %all-to-all-done.1 = f32[64,8,128]{2,1,0:T(8,128)S(1)} async-done(((f32[64,8,128]{2,1,0:T(8,128)}), f32[64,8,128]{2,1,0:T(8,128)S(1)}, u32[]{:S(2)}, u32[]{:S(2)}) %all-to-all-start.1) | async-done | bytes 262176 | tf_op jit(solution)/shard_map/all_to_all | solution.py:33
  69.4 0.1 copy.17
  69.6 0.1 copy.18
  69.8 46.9 %custom-call.7 = f32[4,128,128]{2,1,0:T(8,128)S(1)} custom-call(f32[4,128,128]{2,1,0:T(8,128)S(1)} %fusion.9), custom_call_target="Cholesky" | custom-call | tf_op jit(solution)/shard_map/jit(cholesky)/cholesky | solution.py:70
  116.7 0.1 compare_reduce_fusion
  116.8 0.1 select_bitcast_fusion
  116.9 39.3 %custom-call.8 = f32[4,1,128,128]{2,3,1,0:T(8,128)S(1)} custom-call(f32[4,1,128,128]{3,2,1,0:T(8,128)S(1)} %select_bitcast_fusion), custom_call_target="InvertDiagBlocksLowerTriangular" | custom-call | tf_op jit(solution)/shard_map/triangular_solve | solution.py:71
  156.3 0.6 fusion.7
  156.9 0.6 convolution_multiply_fusion
  157.5 0.2 fusion.18
  157.6 0.2 fusion.17
  157.9 0.2 fusion.16
  158.1 0.2 fusion.15
  158.3 0.7 broadcast_in_dim.48
  159.0 4.2 %all-to-all-start.2 = ((f32[4,128,128]{2,1,0:T(8,128)}), f32[4,128,128]{2,1,0:T(8,128)S(1)}, u32[]{:S(2)}, u32[]{:S(2)}) async-start(f32[4,128,128]{2,1,0:T(8,128)} %broadcast_in_dim.48), calls=%async_computation.2 | async-start | bytes 524288 | tf_op jit(solution)/shard_map/all_to_all | solution.py:33
  163.2 5.7 %all-to-all-done.2 = f32[4,128,128]{2,1,0:T(8,128)S(1)} async-done(((f32[4,128,128]{2,1,0:T(8,128)}), f32[4,128,128]{2,1,0:T(8,128)S(1)}, u32[]{:S(2)}, u32[]{:S(2)}) %all-to-all-start.2) | async-done | bytes 262176 | tf_op jit(solution)/shard_map/all_to_all | solution.py:33
  168.9 0.1 broadcast_select_fusion
  169.0 0.3 fusion.11
  169.3 0.2 fusion.14
  169.5 1.1 while.16
  169.6 0.2 fusion.36
  169.9 0.2 fusion.36
  170.1 0.2 fusion.36
  170.4 0.2 fusion.36
  170.6 5.5 %convolution_convert_fusion = bf16[4,128,4096]{2,1,0:T(8,128)(2,1)} fusion(bf16[4,128,4096]{2,1,0:T(8,128)(2,1)} %param.5, bf16[4,128,128]{2,1,0:T(8,128)(2,1)S(1)} %get-tuple-element.89), kind=kOutput, calls=%fused_computation.8 | convolution fusion | flops 538968064 | bytes 8519680 | tf_op jit(solution)/shard_map/tmn,tmc->tnc/dot_general | solution.py:109
  (19 shorter events, 0.3 us)
Async XLA Ops:
  51.4 18.0 %all-to-all-start.1 = ((f32[64,8,128]{2,1,0:T(8,128)}), f32[64,8,128]{2,1,0:T(8,128)S(1)}, u32[]{:S(2)}, u32[]{:S(2)}) async-start(f32[64,8,128]{2,1,0:T(8,128)} %broadcast_in_dim.46), calls=%async_computation.1 | async-start | bytes 524288 | tf_op jit(solution)/shard_map/all_to_all | solution.py:33
  159.0 9.9 %all-to-all-start.2 = ((f32[4,128,128]{2,1,0:T(8,128)}), f32[4,128,128]{2,1,0:T(8,128)S(1)}, u32[]{:S(2)}, u32[]{:S(2)}) async-start(f32[4,128,128]{2,1,0:T(8,128)} %broadcast_in_dim.48), calls=%async_computation.2 | async-start | bytes 524288 | tf_op jit(solution)/shard_map/all_to_all | solution.py:33
where the time goes:
time: 177 us; the launch traced here: 176 us
  other arithmetic  86.8 us (49%)
  matrix products  34.6 us (20%)
  blocking collectives  24.7 us (14%)
  waiting for transfers between devices  17.5 us (10%)
  starting transfers between devices  10.2 us (6%)
  local copies, waits for them, and re-layouts  1.93 us (1%)
    another operation x3, other arithmetic, transform(): factor = jnp.linalg.cholesky(spread_dof * identity + gram_total)  47.1 us
    another operation x3, other arithmetic, transform(): lax.linalg.triangular_solve(factor, jnp.broadcast_to(identity, gram_total...  39.4 us
    dot_general x1, matrix products, per_device(): jnp.einsum('tmo,tno->tmn', scaled, scaled, preferred_element_type=jnp.flo...  25.9 us
    all_to_all x1, blocking collectives, summed_on_arrival(): blocks = lax.all_to_all(in_blocks(shard, dim, size), axis, 0, 0, tiled=True)  24.7 us
    all_to_all x2, waiting for transfers between devices, copy_for_each(): lax.all_to_all(jnp.broadcast_to(shard[None], (size, *shard.shape)), axis,...  17.5 us
    all_to_all x2, starting transfers between devices, copy_for_each(): lax.all_to_all(jnp.broadcast_to(shard[None], (size, *shard.shape)), axis,...  10.2 us
    dot_general x1, matrix products, per_device(): jnp.einsum('tmn,tmc->tnc', chains_low, anomalies, preferred_element_type=...  5.49 us
  transfers between devices with their start and end apart: 2, of which 2 were waited for; matrix products, arithmetic and copies ran while one was open for 0% of the time, Pallas kernels for 0%

commit v1 on v0

v1 whole, which is shorter than its diff:
```python
import functools

import jax
import jax.numpy as jnp
from jax import lax
from jax.experimental import pallas as pl
from jax.experimental.pallas import tpu as pltpu
from jax.sharding import PartitionSpec as P

M = 128
HALF = 64
LANES = 128
ROWS = 136
HIGHEST = lax.Precision.HIGHEST
NN = (((1,), (0,)), ((), ()))
NT = (((1,), (1,)), ((), ()))
TN = (((0,), (0,)), ((), ()))


def exact_dot(left, right, dims=NN):
    return lax.dot_general(left, right, dims, precision=HIGHEST, preferred_element_type=jnp.float32)


def iota(shape, dim):
    return lax.broadcasted_iota(jnp.int32, shape, dim)


def fold(gram):
    near = jnp.bitwise_and(iota((HALF, M), 1) - iota((HALF, M), 0), M - 1) < HALF
    across = iota((HALF, M), 1) == iota((HALF, M), 0) + HALF
    body = jnp.where(near, gram[:HALF], gram[HALF:])
    rest = jnp.sum(jnp.where(across, gram[:HALF], 0.0), axis=0, keepdims=True)
    return body, rest


def unfold(body, rest):
    near = jnp.bitwise_and(iota((HALF, M), 1) - iota((HALF, M), 0), M - 1) < HALF
    across = iota((HALF, M), 1) == iota((HALF, M), 0) + HALF
    diag = iota((M, M), 0) == iota((M, M), 1)
    top = jnp.where(near, body, jnp.where(across, jnp.broadcast_to(rest, (HALF, M)), 0.0))
    bottom = jnp.where(near, 0.0, body)
    half = jnp.concatenate([top, bottom], axis=0)
    return half + jnp.where(diag, 0.0, half.T)


def gram_kernel(anomalies_ref, index_ref, weight_ref, keep_ref, send_ref):
    time = pl.program_id(0)
    core = lax.rem(lax.axis_index("space"), 2)
    cells = anomalies_ref.shape[2]
    blocks = cells // LANES
    index = index_ref[pl.ds(time, 1), :]
    weight = weight_ref[pl.ds(time, 1), :]
    count = index.shape[1]
    square = weight * weight
    first = square.astype(jnp.bfloat16).astype(jnp.float32)
    second = (square - first).astype(jnp.bfloat16).astype(jnp.float32)
    third = square - first - second
    high = lax.shift_right_logical(index, 7)
    low = jnp.bitwise_and(index, LANES - 1)
    in_block = iota((blocks, count), 0) == high
    rows = jnp.concatenate(
        [jnp.where(in_block, part, 0.0).astype(jnp.bfloat16) for part in (first, second, third)], axis=0
    )
    lanes = jnp.where(iota((LANES, count), 0) == low, 1.0, 0.0).astype(jnp.bfloat16)
    parts = lax.dot_general(rows, lanes, NT, preferred_element_type=jnp.float32)
    total = parts[:blocks] + parts[blocks : 2 * blocks] + parts[2 * blocks :]
    scale = jnp.sqrt(total)
    scaled = jnp.concatenate(
        [
            (
                anomalies_ref[0, :, b * LANES : (b + 1) * LANES].astype(jnp.float32) * scale[b : b + 1, :]
            ).astype(jnp.bfloat16)
            for b in range(blocks)
        ],
        axis=1,
    )
    gram = lax.dot_general(scaled, scaled, NT, preferred_element_type=jnp.float32)
    body, rest = fold(gram)

    def write(ref, second_of_pair):
        start = HALF if second_of_pair else 0
        ref[start : start + HALF, :] = body
        if second_of_pair:
            ref[M + 1 : M + 2, :] = rest
        else:
            ref[M : M + 8, :] = jnp.where(iota((8, M), 0) == 0, jnp.broadcast_to(rest, (8, M)), 0.0)

    for which in range(4):

        @pl.when((time == which) & (core == which // 2))
        def _():
            write(keep_ref, which % 2)

        @pl.when((time == which) & (core != which // 2))
        def _():
            write(send_ref, which % 2)


def gram_parts(anomalies, obs_index, obs_weight):
    times, members, cells = anomalies.shape
    part = jax.ShapeDtypeStruct((ROWS, M), jnp.float32)
    return pl.pallas_call(
        gram_kernel,
        grid=(times,),
        in_specs=[
            pl.BlockSpec((1, members, cells), lambda t: (t, 0, 0)),
            pl.BlockSpec(obs_index.shape, lambda t: (0, 0)),
            pl.BlockSpec(obs_weight.shape, lambda t: (0, 0)),
        ],
        out_specs=[pl.BlockSpec((ROWS, M), lambda t: (0, 0))] * 2,
        out_shape=[part, part],
        name="gram_parts",
    )(anomalies, obs_index, obs_weight)


def invert_halves(panels):
    lane = iota((8, LANES), 1)
    column = jnp.bitwise_and(lane, HALF - 1)
    first_lane = lane - column
    row = iota((8, LANES), 0)

    def column_of(panel, k):
        return jnp.take_along_axis(panel, first_lane + k, axis=1)

    def row_of(panel, k):
        return jnp.broadcast_to(panel[k : k + 1, :], panel.shape)

    for start in range(0, HALF, 4):
        own, offset = start // 8, start % 8
        rows = [row_of(panels[own], offset + j) for j in range(4)]
        columns = [column_of(panels[own], start + j) for j in range(4)]

        def at(i, j):
            return row_of(columns[j], offset + i)

        e11, e12, e22 = at(0, 0), at(0, 1), at(1, 1)
        f11, f12, f21, f22 = at(0, 2), at(0, 3), at(1, 2), at(1, 3)
        h11, h12, h22 = at(2, 2), at(2, 3), at(3, 3)
        d = 1.0 / (e11 * e22 - e12 * e12)
        x11, x12 = (e22 * f11 - e12 * f21) * d, (e22 * f12 - e12 * f22) * d
        x21, x22 = (e11 * f21 - e12 * f11) * d, (e11 * f22 - e12 * f12) * d
        s11 = h11 - (f11 * x11 + f21 * x21)
        s12 = h12 - (f11 * x12 + f21 * x22)
        s22 = h22 - (f12 * x12 + f22 * x22)
        g = 1.0 / (s11 * s22 - s12 * s12)
        m33, m34, m44 = s22 * g, -s12 * g, s11 * g
        m13, m14 = -(x11 * m33 + x12 * m34), -(x11 * m34 + x12 * m44)
        m23, m24 = -(x21 * m33 + x22 * m34), -(x21 * m34 + x22 * m44)
        m11 = e22 * d - (m13 * x11 + m14 * x12)
        m12 = -e12 * d - (m13 * x21 + m14 * x22)
        m22 = e11 * d - (m23 * x21 + m24 * x22)
        inverse = (
            (m11, m12, m13, m14),
            (m12, m22, m23, m24),
            (m13, m23, m33, m34),
            (m14, m24, m34, m44),
        )
        pivots = (column >= start) & (column < start + 4)
        rows = [jnp.where(pivots, jnp.where(column == start + j, 1.0, 0.0), rows[j]) for j in range(4)]
        solved = [
            (line[0] * rows[0] + line[1] * rows[1]) + (line[2] * rows[2] + line[3] * rows[3]) for line in inverse
        ]
        result = list(panels)
        for p in [(own + 1 + q) % 8 for q in range(8)]:
            out = jnp.where(pivots, 0.0, panels[p])
            for j in range(4):
                out = out - (columns[j] if p == own else column_of(panels[p], start + j)) * solved[j]
            if p == own:
                for i in range(4):
                    out = jnp.where(row == offset + i, solved[i], out)
            result[p] = out
        panels = result
    return panels


def invert_packed(packed):
    return jnp.concatenate(invert_halves([packed[8 * p : 8 * p + 8] for p in range(8)]), axis=0)


def invert_pair(pair):
    left = iota((HALF, M), 1) < HALF
    corner = iota((HALF, M), 1) == iota((HALF, M), 0) + HALF
    one, two = pair
    first = invert_packed(jnp.where(left, one[:HALF], pltpu.roll(two[:HALF], HALF, 1)))
    firsts = (first, pltpu.roll(first, HALF, 1))
    crosses = [exact_dot(g[HALF:, :HALF], f[:, :HALF]) for g, f in zip(pair, firsts)]
    schur = [g[HALF:] - exact_dot(x, g[:HALF]) for g, x in zip(pair, crosses)]
    second = invert_packed(jnp.where(left, pltpu.roll(schur[0], HALF, 1), schur[1]))
    seconds = (second, pltpu.roll(second, HALF, 1))
    inverses = []
    for f, x, s in zip(firsts, crosses, seconds):
        border = jnp.concatenate([x, jnp.zeros((HALF, HALF), jnp.float32)], axis=1) - jnp.where(corner, 1.0, 0.0)
        whole = exact_dot(border, exact_dot(s[:, :HALF], border), TN)
        inverses.append(jnp.concatenate([whole[:HALF] + jnp.where(left, f, 0.0), whole[HALF:]], axis=0))
    return inverses


def weights_kernel(parts_ref, out_ref):
    dof = float(M - 1)
    total = parts_ref[0]
    for k in range(1, parts_ref.shape[0]):
        total = total + parts_ref[k]
    diag = jnp.where(iota((M, M), 0) == iota((M, M), 1), dof, 0.0)
    pair = [
        unfold(total[HALF * k : HALF * k + HALF], total[M + k : M + k + 1]) + diag for k in range(2)
    ]
    first, second = (dof * w for w in invert_pair(pair))
    out_ref[:M, :] = second
    out_ref[M:, :] = exact_dot(first, second)


def weights_of(parts):
    return pl.pallas_call(
        weights_kernel,
        out_shape=jax.ShapeDtypeStruct((2 * M, M), jnp.float32),
        name="weights",
    )(parts)


def products_kernel(own_ref, other_ref, product_ref, factors_ref):
    core = lax.rem(lax.axis_index("space"), 2)
    own, other = own_ref[...], other_ref[...]
    early = jnp.where(core == 0, own, other)
    late = jnp.where(core == 0, other, own)
    product_ref[...] = exact_dot(early[M:], late[M:])
    factors_ref[: 2 * M, :] = late
    factors_ref[2 * M :, :] = exact_dot(early[:M], late[M:])


def products_of(own, other):
    return pl.pallas_call(
        products_kernel,
        out_shape=[
            jax.ShapeDtypeStruct((M, M), jnp.float32),
            jax.ShapeDtypeStruct((3 * M, M), jnp.float32),
        ],
        name="products",
    )(own, other)


def smooth_kernel(one_ref, two_ref, three_ref, factors_ref, anomalies_ref, out_ref, chains_ref):
    @pl.when(pl.program_id(0) == 0)
    def _():
        position = lax.axis_index("tm")
        eye = jnp.where(iota((M, M), 0) == iota((M, M), 1), 1.0, 0.0)
        later = [
            jnp.where(position + k < 4, ref[...], eye)
            for k, ref in ((1, one_ref), (2, two_ref), (3, three_ref))
        ]
        suffix = exact_dot(later[0], exact_dot(later[1], later[2]))
        chains_ref[3] = suffix.T.astype(jnp.bfloat16)
        earlier = exact_dot(factors_ref[...], suffix)
        for k in range(3):
            chains_ref[2 - k] = earlier[M * k : M * k + M].T.astype(jnp.bfloat16)

    out_ref[0] = jnp.dot(
        chains_ref[pl.program_id(0)], anomalies_ref[0], preferred_element_type=jnp.float32
    ).astype(jnp.bfloat16)


def smooth(later, factors, anomalies):
    times, members, cells = anomalies.shape
    whole = pl.BlockSpec((M, M), lambda t: (0, 0))
    block = pl.BlockSpec((1, members, cells), lambda t: (t, 0, 0))
    return pl.pallas_call(
        smooth_kernel,
        grid=(times,),
        in_specs=[whole, whole, whole, pl.BlockSpec((3 * M, M), lambda t: (0, 0)), block],
        out_specs=block,
        out_shape=jax.ShapeDtypeStruct(anomalies.shape, jnp.bfloat16),
        scratch_shapes=[pltpu.VMEM((4, M, M), jnp.bfloat16)],
        name="smooth",
    )(*later, factors, anomalies)


XS, ZS, CORES = 4, 8, 2


def place(x, z, core):
    return ((x % XS) * ZS + z % ZS) * CORES + core % CORES


def sites():
    return [(x, z, c) for x in range(XS) for z in range(ZS) for c in range(CORES)]


def per_device(anomalies, obs_index, obs_weight):
    swap = [(place(*s), place(s[0], s[1], s[2] + 1)) for s in sites()]
    keep, send = gram_parts(anomalies, obs_index, obs_weight)
    part = keep + lax.ppermute(send, "space", swap)
    around = [
        lax.ppermute(part, "space", [(place(*s), place(s[0] + k, s[1], s[2])) for s in sites()])
        for k in range(1, XS)
    ]
    part = part + around[0] + around[1] + around[2]
    groups = [[place(x, z, c) for z in range(ZS)] for x in range(XS) for c in range(CORES)]
    parts = lax.all_to_all(
        jnp.broadcast_to(part[None], (ZS, ROWS, M)), "space", 0, 0, axis_index_groups=groups, tiled=True
    )
    own = weights_of(parts)
    product, factors = products_of(own, lax.ppermute(own, "space", swap))
    later = [lax.ppermute(product, "tm", [(g, (g - k) % 4) for g in range(4)]) for k in range(1, 4)]
    return smooth(later, factors, anomalies)


def solution(mesh):
    return jax.shard_map(
        per_device,
        mesh=mesh,
        in_specs=(P("tm", None, "space"), P("tm", "space"), P("tm", "space")),
        out_specs=P("tm", None, "space"),
        check_vma=False,
    )
```

time: 177 us -> 72.3 us (0.41)
  other arithmetic: 86.8 us -> 0.92 us
  matrix products: 34.6 us -> 0 us
  Pallas kernels: 0 us -> 22 us
  waiting for transfers between devices: 17.5 us -> 10.4 us
  starting transfers between devices: 10.2 us -> 13.1 us
    another operation x6 -> x0, other arithmetic: 86.5 us -> none  [the longest x3 47.1 us: transform(): factor = jnp.linalg.cholesky(spread_dof * identity + gram_total)]
    dot_general x13 -> x0, matrix products: 34 us -> none  [the longest x1 25.9 us: per_device(): jnp.einsum('tmo,tno->tmn', scaled, scaled, preferred_element_type=jnp.flo...]
    pallas_call x0 -> x4, Pallas kernels: none -> 22 us  [the longest x1 7.9 us: weights_of(): pl.pallas_call(weights_kernel, out_shape=jax.ShapeDtypeStruct((2 * M, M),...]
    all_to_all x2 -> x0, waiting for transfers between devices: 17.5 us -> none  [copy_for_each(): lax.all_to_all(jnp.broadcast_to(shard[None], (size, *shard.shape)), axis,...]
    ppermute x0 -> x8, starting transfers between devices: none -> 13.1 us  [the longest x3 4.97 us: per_device(): lax.ppermute(product, 'tm', [(g, (g - k) % 4) for g in range(4)])]
    ppermute x0 -> x8, waiting for transfers between devices: none -> 10.4 us  [the longest x3 5.56 us: per_device(): lax.ppermute(part, 'space', [(place(*s), place(s[0] + k, s[1], s[2])) for...]
    all_to_all x2 -> x0, starting transfers between devices: 10.2 us -> none  [copy_for_each(): lax.all_to_all(jnp.broadcast_to(shard[None], (size, *shard.shape)), axis,...]
  transfers between devices with their start and end apart: 2 -> 8, of which waited for: 2 -> 7; matrix products, arithmetic and copies ran while one was open for 0% -> 0% of each run, Pallas kernels for 0% -> 0%
where the time goes in v1:
time: 72.3 us; the launch traced here: 72 us
  blocking collectives  24.2 us (33%)
  Pallas kernels  22 us (30%)
  starting transfers between devices  13.1 us (18%)
  waiting for transfers between devices  10.4 us (14%)
  local copies, waits for them, and re-layouts  1.3 us (2%)
  other arithmetic  0.92 us (1%)
    all_to_all x1, blocking collectives, per_device(): lax.all_to_all(jnp.broadcast_to(part[None], (ZS, ROWS, M)), 'space', 0, 0...  24.2 us
    pallas_call x1, Pallas kernels, weights_of(): pl.pallas_call(weights_kernel, out_shape=jax.ShapeDtypeStruct((2 * M, M),...  7.9 us
    pallas_call x1, Pallas kernels, smooth(): pl.pallas_call(smooth_kernel, grid=(times,), in_specs=[whole, whole, whol...  6.41 us
    pallas_call x1, Pallas kernels, gram_parts(): pl.pallas_call(gram_kernel, grid=(times,), in_specs=[pl.BlockSpec((1, mem...  5.75 us
    ppermute x3, waiting for transfers between devices, per_device(): lax.ppermute(part, 'space', [(place(*s), place(s[0] + k, s[1], s[2])) for...  5.56 us
    ppermute x3, starting transfers between devices, per_device(): lax.ppermute(product, 'tm', [(g, (g - k) % 4) for g in range(4)])  4.97 us
    ppermute x1, starting transfers between devices, per_device(): part = keep + lax.ppermute(send, 'space', swap)  3.2 us
    ppermute x1, starting transfers between devices, per_device(): product, factors = products_of(own, lax.ppermute(own, 'space', swap))  2.91 us
  transfers between devices with their start and end apart: 8, of which 7 were waited for; matrix products, arithmetic and copies ran while one was open for 0% of the time, Pallas kernels for 0%

profile of v1, /device:TPU:1, one launch (start us, length us, event | category | flops | bytes accessed | tf_op | source)
XLA Modules:
  0.0 72.0 jit_solution(3165958383152827331)
XLA Ops:
  0.0 5.7 %gram_parts.1 = (f32[136,128]{1,0:T(8,128)}, f32[136,128]{1,0:T(8,128)}) custom-call(bf16[4,128,4096]{2,1,0:T(8,128)(2,1)} %anomalies_ref.3, s32[4,1024]{1,0:T(4,128)} %index_ref.1, f32[4,1024]{1,0:T(4,128)} %weight_ref.1), custom_call_target="tpu_custom_call" | custom-call | tf_op jit(solution)/shard_map/gram_parts/pallas_call | solution.py:102
  5.8 3.2 %collective-permute-start = (f32[136,128]{1,0:T(8,128)}, f32[136,128]{1,0:T(8,128)S(1)}, u32[]{:S(2)}, u32[]{:S(2)}) collective-permute-start(f32[136,128]{1,0:T(8,128)} %get-tuple-element.10), channel_id=1, source_target_pairs={{0,1},{1,0},{2,3},{3,2},{4,5},{5,4},{6,7},{7,6},{8,9},{9,8},{10,11... | collective-permute-start | bytes 208904 | tf_op jit(solution)/shard_map/ppermute | solution.py:290
  8.9 1.1 %collective-permute-done = f32[136,128]{1,0:T(8,128)S(1)} collective-permute-done((f32[136,128]{1,0:T(8,128)}, f32[136,128]{1,0:T(8,128)S(1)}, u32[]{:S(2)}, u32[]{:S(2)}) %collective-permute-start) | collective-permute-done | bytes 69664 | tf_op jit(solution)/shard_map/ppermute | solution.py:290
  10.1 0.9 %add.12 = f32[136,128]{1,0:T(8,128)S(1)} add(f32[136,128]{1,0:T(8,128)} %get-tuple-element.9, f32[136,128]{1,0:T(8,128)S(1)} %collective-permute-done) | non-fusion elementwise | flops 17408 | bytes 208896 | tf_op jit(solution)/shard_map/add | solution.py:290
  11.0 0.8 %collective-permute-start.3 = (f32[136,128]{1,0:T(8,128)S(1)}, f32[136,128]{1,0:T(8,128)S(1)}, u32[]{:S(2)}, u32[]{:S(2)}) collective-permute-start(f32[136,128]{1,0:T(8,128)S(1)} %add.12), channel_id=1, source_target_pairs={{0,48},{1,49},{2,50},{3,51},{4,52},{5,53},{6,54},{7,55},{8,56},{9,... | collective-permute-start | bytes 208904 | tf_op jit(solution)/shard_map/ppermute | solution.py:292
  11.8 0.5 collective-permute-start.2
  12.3 0.6 collective-permute-start.1
  12.9 1.3 %collective-permute-done.3 = f32[136,128]{1,0:T(8,128)S(1)} collective-permute-done((f32[136,128]{1,0:T(8,128)S(1)}, f32[136,128]{1,0:T(8,128)S(1)}, u32[]{:S(2)}, u32[]{:S(2)}) %collective-permute-start.3) | collective-permute-done | bytes 69664 | tf_op jit(solution)/shard_map/ppermute | solution.py:292
  14.2 2.3 %collective-permute-done.2 = f32[136,128]{1,0:T(8,128)S(1)} collective-permute-done((f32[136,128]{1,0:T(8,128)S(1)}, f32[136,128]{1,0:T(8,128)S(1)}, u32[]{:S(2)}, u32[]{:S(2)}) %collective-permute-start.2) | collective-permute-done | bytes 69664 | tf_op jit(solution)/shard_map/ppermute | solution.py:292
  16.5 2.0 %collective-permute-done.1 = f32[136,128]{1,0:T(8,128)S(1)} collective-permute-done((f32[136,128]{1,0:T(8,128)S(1)}, f32[136,128]{1,0:T(8,128)S(1)}, u32[]{:S(2)}, u32[]{:S(2)}) %collective-permute-start.1) | collective-permute-done | bytes 69664 | tf_op jit(solution)/shard_map/ppermute | solution.py:292
  18.6 24.2 %all_to_all.5.parts_ref = f32[8,136,128]{2,1,0:T(8,128)} all-to-all(f32[8,136,128]{2,1,0:T(8,128)S(1)} %broadcast_in_dim.2), channel_id=1, replica_groups={{0,2,4,6,8,10,12,14},{1,3,5,7,9,11,13,15},{16,18,20,22,24,26,28,30},{17..., dimensions={0} | all-to-all | bytes 1114112 | tf_op jit(solution)/shard_map/all_to_all | solution.py:297
  42.8 7.9 %weights.1.own_ref = f32[256,128]{1,0:T(8,128)} custom-call(f32[8,136,128]{2,1,0:T(8,128)} %all_to_all.5.parts_ref), custom_call_target="tpu_custom_call" | custom-call | tf_op jit(solution)/shard_map/weights/pallas_call | solution.py:213
  50.7 2.9 %collective-permute-start.4 = (f32[256,128]{1,0:T(8,128)}, f32[256,128]{1,0:T(8,128)S(1)}, u32[]{:S(2)}, u32[]{:S(2)}) collective-permute-start(f32[256,128]{1,0:T(8,128)} %weights.1.own_ref), channel_id=1, source_target_pairs={{0,1},{1,0},{2,3},{3,2},{4,5},{5,4},{6,7},{7,6},{8,9},{9,8},{10,11... | collective-permute-start | bytes 393224 | tf_op jit(solution)/shard_map/ppermute | solution.py:301
  53.6 1.2 %collective-permute-done.4.other_ref = f32[256,128]{1,0:T(8,128)S(1)} collective-permute-done((f32[256,128]{1,0:T(8,128)}, f32[256,128]{1,0:T(8,128)S(1)}, u32[]{:S(2)}, u32[]{:S(2)}) %collective-permute-start.4) | collective-permute-done | bytes 131104 | tf_op jit(solution)/shard_map/ppermute | solution.py:301
  54.8 0.0 copy-start
  54.8 0.6 copy-done
  55.5 2.0 %products.1 = (f32[128,128]{1,0:T(8,128)}, f32[384,128]{1,0:T(8,128)}) custom-call(f32[256,128]{1,0:T(8,128)} %weights.1.own_ref, f32[256,128]{1,0:T(8,128)} %copy-done), custom_call_target="tpu_custom_call" | custom-call | tf_op jit(solution)/shard_map/products/pallas_call | solution.py:231
  57.4 1.3 %collective-permute-start.7 = (f32[128,128]{1,0:T(8,128)}, f32[128,128]{1,0:T(8,128)S(1)}, u32[]{:S(2)}, u32[]{:S(2)}) collective-permute-start(f32[128,128]{1,0:T(8,128)} %get-tuple-element.11), channel_id=1, source_target_pairs={{0,64},{64,128},{128,192},{192,0},{1,65},{65,129},{129,193},{193,1... | collective-permute-start | bytes 196616 | tf_op jit(solution)/shard_map/ppermute | solution.py:302
  58.7 2.6 %collective-permute-start.6 = (f32[128,128]{1,0:T(8,128)}, f32[128,128]{1,0:T(8,128)S(1)}, u32[]{:S(2)}, u32[]{:S(2)}) collective-permute-start(f32[128,128]{1,0:T(8,128)} %get-tuple-element.11), channel_id=1, source_target_pairs={{0,128},{64,192},{128,0},{192,64},{1,129},{65,193},{129,1},{193,65... | collective-permute-start | bytes 196616 | tf_op jit(solution)/shard_map/ppermute | solution.py:302
  61.3 1.1 %collective-permute-start.5 = (f32[128,128]{1,0:T(8,128)}, f32[128,128]{1,0:T(8,128)S(1)}, u32[]{:S(2)}, u32[]{:S(2)}) collective-permute-start(f32[128,128]{1,0:T(8,128)} %get-tuple-element.11), channel_id=1, source_target_pairs={{0,192},{64,0},{128,64},{192,128},{1,193},{65,1},{129,65},{193,129... | collective-permute-start | bytes 196616 | tf_op jit(solution)/shard_map/ppermute | solution.py:302
  62.4 0.0 collective-permute-done.7.three_ref
  62.4 0.0 copy-start.1
  62.4 2.1 %collective-permute-done.6.two_ref = f32[128,128]{1,0:T(8,128)S(1)} collective-permute-done((f32[128,128]{1,0:T(8,128)}, f32[128,128]{1,0:T(8,128)S(1)}, u32[]{:S(2)}, u32[]{:S(2)}) %collective-permute-start.6) | collective-permute-done | bytes 65568 | tf_op jit(solution)/shard_map/ppermute | solution.py:302
  64.5 0.0 copy-start.2
  64.5 0.5 collective-permute-done.5.one_ref
  64.9 0.0 copy-start.3
  64.9 0.0 copy-done.1
  64.9 0.1 copy-done.2
  65.1 0.5 copy-done.3
  65.6 6.4 %smooth.1 = bf16[4,128,4096]{2,1,0:T(8,128)(2,1)} custom-call(f32[128,128]{1,0:T(8,128)} %copy-done.3, f32[128,128]{1,0:T(8,128)} %copy-done.2, f32[128,128]{1,0:T(8,128)} %copy-done.1, f32[384,128]{1,0:T(8,128)} %get-tuple-element.12.factors_ref, bf16[4,128,4096]{2,1,0:T(8,128)(2,1)} %anomalies_ref.3), custom_call_target="tpu_custom_call" | custom-call | tf_op jit(solution)/shard_map/smooth/pallas_call | solution.py:265
  (2 shorter events, 0.1 us)
Async XLA Ops:
  5.8 4.3 %collective-permute-start = (f32[136,128]{1,0:T(8,128)}, f32[136,128]{1,0:T(8,128)S(1)}, u32[]{:S(2)}, u32[]{:S(2)}) collective-permute-start(f32[136,128]{1,0:T(8,128)} %get-tuple-element.10), channel_id=1, source_target_pairs={{0,1},{1,0},{2,3},{3,2},{4,5},{5,4},{6,7},{7,6},{8,9},{9,8},{10,11... | collective-permute-start | bytes 208904 | tf_op jit(solution)/shard_map/ppermute | solution.py:290
  11.0 3.2 %collective-permute-start.3 = (f32[136,128]{1,0:T(8,128)S(1)}, f32[136,128]{1,0:T(8,128)S(1)}, u32[]{:S(2)}, u32[]{:S(2)}) collective-permute-start(f32[136,128]{1,0:T(8,128)S(1)} %add.12), channel_id=1, source_target_pairs={{0,48},{1,49},{2,50},{3,51},{4,52},{5,53},{6,54},{7,55},{8,56},{9,... | collective-permute-start | bytes 208904 | tf_op jit(solution)/shard_map/ppermute | solution.py:292
  11.8 4.7 %collective-permute-start.2 = (f32[136,128]{1,0:T(8,128)S(1)}, f32[136,128]{1,0:T(8,128)S(1)}, u32[]{:S(2)}, u32[]{:S(2)}) collective-permute-start(f32[136,128]{1,0:T(8,128)S(1)} %add.12), channel_id=1, source_target_pairs={{0,32},{1,33},{2,34},{3,35},{4,36},{5,37},{6,38},{7,39},{8,40},{9,... | collective-permute-start | bytes 208904 | tf_op jit(solution)/shard_map/ppermute | solution.py:292
  12.3 6.2 %collective-permute-start.1 = (f32[136,128]{1,0:T(8,128)S(1)}, f32[136,128]{1,0:T(8,128)S(1)}, u32[]{:S(2)}, u32[]{:S(2)}) collective-permute-start(f32[136,128]{1,0:T(8,128)S(1)} %add.12), channel_id=1, source_target_pairs={{0,16},{1,17},{2,18},{3,19},{4,20},{5,21},{6,22},{7,23},{8,24},{9,... | collective-permute-start | bytes 208904 | tf_op jit(solution)/shard_map/ppermute | solution.py:292
  50.7 4.1 %collective-permute-start.4 = (f32[256,128]{1,0:T(8,128)}, f32[256,128]{1,0:T(8,128)S(1)}, u32[]{:S(2)}, u32[]{:S(2)}) collective-permute-start(f32[256,128]{1,0:T(8,128)} %weights.1.own_ref), channel_id=1, source_target_pairs={{0,1},{1,0},{2,3},{3,2},{4,5},{5,4},{6,7},{7,6},{8,9},{9,8},{10,11... | collective-permute-start | bytes 393224 | tf_op jit(solution)/shard_map/ppermute | solution.py:301
  54.8 0.6 copy-start
  57.4 5.0 %collective-permute-start.7 = (f32[128,128]{1,0:T(8,128)}, f32[128,128]{1,0:T(8,128)S(1)}, u32[]{:S(2)}, u32[]{:S(2)}) collective-permute-start(f32[128,128]{1,0:T(8,128)} %get-tuple-element.11), channel_id=1, source_target_pairs={{0,64},{64,128},{128,192},{192,0},{1,65},{65,129},{129,193},{193,1... | collective-permute-start | bytes 196616 | tf_op jit(solution)/shard_map/ppermute | solution.py:302
  58.7 5.8 %collective-permute-start.6 = (f32[128,128]{1,0:T(8,128)}, f32[128,128]{1,0:T(8,128)S(1)}, u32[]{:S(2)}, u32[]{:S(2)}) collective-permute-start(f32[128,128]{1,0:T(8,128)} %get-tuple-element.11), channel_id=1, source_target_pairs={{0,128},{64,192},{128,0},{192,64},{1,129},{65,193},{129,1},{193,65... | collective-permute-start | bytes 196616 | tf_op jit(solution)/shard_map/ppermute | solution.py:302
  61.3 3.6 %collective-permute-start.5 = (f32[128,128]{1,0:T(8,128)}, f32[128,128]{1,0:T(8,128)S(1)}, u32[]{:S(2)}, u32[]{:S(2)}) collective-permute-start(f32[128,128]{1,0:T(8,128)} %get-tuple-element.11), channel_id=1, source_target_pairs={{0,192},{64,0},{128,64},{192,128},{1,193},{65,1},{129,65},{193,129... | collective-permute-start | bytes 196616 | tf_op jit(solution)/shard_map/ppermute | solution.py:302
  62.4 2.6 %copy-start.1 = (f32[128,128]{1,0:T(8,128)}, f32[128,128]{1,0:T(8,128)S(1)}, u32[]{:S(2)}) copy-start(f32[128,128]{1,0:T(8,128)S(1)} %collective-permute-done.7.three_ref) | copy-start | bytes 196612
  64.5 0.6 copy-start.2
  64.9 0.6 copy-start.3

commit v2 on v1

--- a/solution.py
+++ b/solution.py
@@ -1,5 +1,3 @@
-import functools
-
 import jax
 import jax.numpy as jnp
 from jax import lax
@@ -43,13 +41,7 @@
     return half + jnp.where(diag, 0.0, half.T)
 
 
-def gram_kernel(anomalies_ref, index_ref, weight_ref, keep_ref, send_ref):
-    time = pl.program_id(0)
-    core = lax.rem(lax.axis_index("space"), 2)
-    cells = anomalies_ref.shape[2]
-    blocks = cells // LANES
-    index = index_ref[pl.ds(time, 1), :]
-    weight = weight_ref[pl.ds(time, 1), :]
+def cell_scales(index, weight, blocks):
     count = index.shape[1]
     square = weight * weight
     first = square.astype(jnp.bfloat16).astype(jnp.float32)
@@ -63,54 +55,98 @@
     )
     lanes = jnp.where(iota((LANES, count), 0) == low, 1.0, 0.0).astype(jnp.bfloat16)
     parts = lax.dot_general(rows, lanes, NT, preferred_element_type=jnp.float32)
-    total = parts[:blocks] + parts[blocks : 2 * blocks] + parts[2 * blocks :]
-    scale = jnp.sqrt(total)
-    scaled = jnp.concatenate(
-        [
-            (
-                anomalies_ref[0, :, b * LANES : (b + 1) * LANES].astype(jnp.float32) * scale[b : b + 1, :]
-            ).astype(jnp.bfloat16)
-            for b in range(blocks)
+    return jnp.sqrt(parts[:blocks] + parts[blocks : 2 * blocks] + parts[2 * blocks :])
+
+
+def write_grams(first, held_ref, index_ref, weight_ref, part_ref, arrived):
+    blocks = held_ref.shape[2] // LANES
+    scales = [
+        cell_scales(index_ref[pl.ds(first + k, 1), :], weight_ref[pl.ds(first + k, 1), :], blocks)
+        for k in range(2)
+    ]
+    rests = []
+    for k in range(2):
+        arrived(k)
+        scaled = jnp.concatenate(
+            [
+                (
+                    held_ref[first + k, :, b * LANES : (b + 1) * LANES].astype(jnp.float32)
+                    * scales[k][b : b + 1, :]
+                ).astype(jnp.bfloat16)
+                for b in range(blocks)
+            ],
+            axis=1,
+        )
+        gram = lax.dot_general(scaled, scaled, NT, preferred_element_type=jnp.float32)
+        body, rest = fold(gram)
+        part_ref[HALF * k : HALF * k + HALF, :] = body
+        rests.append(jnp.broadcast_to(rest, (8, M)))
+    row = iota((8, M), 0)
+    part_ref[M:, :] = jnp.where(row == 0, rests[0], jnp.where(row == 1, rests[1], 0.0))
+
+
+def gram_other_kernel(anomalies_ref, index_ref, weight_ref, part_ref, held_ref, index_held, weight_held, sems):
+    core = lax.rem(lax.axis_index("space"), 2)
+    order = [2 * (1 - core), 2 * (1 - core) + 1, 2 * core, 2 * core + 1]
+    small = [
+        pltpu.make_async_copy(index_ref, index_held, sems.at[0]),
+        pltpu.make_async_copy(weight_ref, weight_held, sems.at[1]),
+    ]
+    large = [
+        pltpu.make_async_copy(anomalies_ref.at[t], held_ref.at[t], sems.at[2 + k]) for k, t in enumerate(order)
+    ]
+    for copy in small + large:
+        copy.start()
+    for copy in small:
+        copy.wait()
+    write_grams(order[0], held_ref, index_held, weight_held, part_ref, lambda k: large[k].wait())
+    for copy in large[2:]:
+        copy.wait()
+
+
+def gram_own_kernel(held_ref, index_ref, weight_ref, part_ref):
+    core = lax.rem(lax.axis_index("space"), 2)
+    write_grams(2 * core, held_ref, index_ref, weight_ref, part_ref, lambda k: None)
+
+
+HBM = pl.BlockSpec(memory_space=pltpu.HBM)
+VMEM = pl.BlockSpec(memory_space=pltpu.VMEM)
+
+
+def gram_cost(anomalies):
+    times, members, cells = anomalies.shape
+    return pl.CostEstimate(
+        flops=times * members * members * cells, bytes_accessed=times * members * cells, transcendentals=0
+    )
+
+
+def gram_other(anomalies, obs_index, obs_weight):
+    inputs = (anomalies, obs_index, obs_weight)
+    return pl.pallas_call(
+        gram_other_kernel,
+        in_specs=[HBM] * 3,
+        out_specs=[VMEM] * 4,
+        out_shape=[
+            jax.ShapeDtypeStruct((ROWS, M), jnp.float32),
+            *(jax.ShapeDtypeStruct(x.shape, x.dtype) for x in inputs),
         ],
-        axis=1,
-    )
-    gram = lax.dot_general(scaled, scaled, NT, preferred_element_type=jnp.float32)
-    body, rest = fold(gram)
-
-    def write(ref, second_of_pair):
-        start = HALF if second_of_pair else 0
-        ref[start : start + HALF, :] = body
-        if second_of_pair:
-            ref[M + 1 : M + 2, :] = rest
-        else:
-            ref[M : M + 8, :] = jnp.where(iota((8, M), 0) == 0, jnp.broadcast_to(rest, (8, M)), 0.0)
-
-    for which in range(4):
-
-        @pl.when((time == which) & (core == which // 2))
-        def _():
-            write(keep_ref, which % 2)
-
-        @pl.when((time == which) & (core != which // 2))
-        def _():
-            write(send_ref, which % 2)
-
-
-def gram_parts(anomalies, obs_index, obs_weight):
-    times, members, cells = anomalies.shape
-    part = jax.ShapeDtypeStruct((ROWS, M), jnp.float32)
-    return pl.pallas_call(
-        gram_kernel,
-        grid=(times,),
-        in_specs=[
-            pl.BlockSpec((1, members, cells), lambda t: (t, 0, 0)),
-            pl.BlockSpec(obs_index.shape, lambda t: (0, 0)),
-            pl.BlockSpec(obs_weight.shape, lambda t: (0, 0)),
-        ],
-        out_specs=[pl.BlockSpec((ROWS, M), lambda t: (0, 0))] * 2,
-        out_shape=[part, part],
-        name="gram_parts",
-    )(anomalies, obs_index, obs_weight)
+        scratch_shapes=[pltpu.SemaphoreType.DMA((6,))],
+        compiler_params=pltpu.CompilerParams(vmem_limit_bytes=12 << 20),
+        cost_estimate=gram_cost(anomalies),
+        name="gram_other",
+    )(*(pltpu.with_memory_space_constraint(x, pltpu.HBM) for x in inputs))
+
+
+def gram_own(held, obs_index, obs_weight):
+    return pl.pallas_call(
+        gram_own_kernel,
+        in_specs=[VMEM] * 3,
+        out_specs=VMEM,
+        out_shape=jax.ShapeDtypeStruct((ROWS, M), jnp.float32),
+        compiler_params=pltpu.CompilerParams(vmem_limit_bytes=12 << 20),
+        cost_estimate=gram_cost(held),
+        name="gram_own",
+    )(held, obs_index, obs_weight)
 
 
 def invert_halves(panels):
@@ -161,10 +197,14 @@
             (line[0] * rows[0] + line[1] * rows[1]) + (line[2] * rows[2] + line[3] * rows[3]) for line in inverse
         ]
         result = list(panels)
-        for p in [(own + 1 + q) % 8 for q in range(8)]:
+        order = [(own + (start % 8 == 4) + q) % 8 for q in range(8)]
+        spread = [
+            {p: columns[j] if p == own else column_of(panels[p], start + j) for p in order} for j in range(4)
+        ]
+        for p in order:
             out = jnp.where(pivots, 0.0, panels[p])
             for j in range(4):
-                out = out - (columns[j] if p == own else column_of(panels[p], start + j)) * solved[j]
+                out = out - spread[j][p] * solved[j]
             if p == own:
                 for i in range(4):
                     out = jnp.where(row == offset + i, solved[i], out)
@@ -213,6 +253,7 @@
     return pl.pallas_call(
         weights_kernel,
         out_shape=jax.ShapeDtypeStruct((2 * M, M), jnp.float32),
+        compiler_params=pltpu.CompilerParams(vmem_limit_bytes=4 << 20),
         name="weights",
     )(parts)
 
@@ -234,43 +275,56 @@
             jax.ShapeDtypeStruct((M, M), jnp.float32),
             jax.ShapeDtypeStruct((3 * M, M), jnp.float32),
         ],
+        compiler_params=pltpu.CompilerParams(vmem_limit_bytes=4 << 20),
         name="products",
     )(own, other)
 
 
-def smooth_kernel(one_ref, two_ref, three_ref, factors_ref, anomalies_ref, out_ref, chains_ref):
-    @pl.when(pl.program_id(0) == 0)
-    def _():
-        position = lax.axis_index("tm")
-        eye = jnp.where(iota((M, M), 0) == iota((M, M), 1), 1.0, 0.0)
-        later = [
-            jnp.where(position + k < 4, ref[...], eye)
-            for k, ref in ((1, one_ref), (2, two_ref), (3, three_ref))
-        ]
-        suffix = exact_dot(later[0], exact_dot(later[1], later[2]))
-        chains_ref[3] = suffix.T.astype(jnp.bfloat16)
-        earlier = exact_dot(factors_ref[...], suffix)
-        for k in range(3):
-            chains_ref[2 - k] = earlier[M * k : M * k + M].T.astype(jnp.bfloat16)
-
-    out_ref[0] = jnp.dot(
-        chains_ref[pl.program_id(0)], anomalies_ref[0], preferred_element_type=jnp.float32
-    ).astype(jnp.bfloat16)
-
-
-def smooth(later, factors, anomalies):
-    times, members, cells = anomalies.shape
-    whole = pl.BlockSpec((M, M), lambda t: (0, 0))
-    block = pl.BlockSpec((1, members, cells), lambda t: (t, 0, 0))
+def smooth_kernel(one_ref, two_ref, three_ref, factors_ref, held_ref, out_ref, staged_ref, sems):
+    position = lax.axis_index("tm")
+    eye = jnp.where(iota((M, M), 0) == iota((M, M), 1), 1.0, 0.0)
+    later = [
+        jnp.where(position + k < 4, ref[...], eye) for k, ref in ((1, one_ref), (2, two_ref), (3, three_ref))
+    ]
+    suffix = exact_dot(later[0], exact_dot(later[1], later[2]))
+    copies = []
+
+    def write(time, chain):
+        chain = chain.T.astype(jnp.bfloat16)
+        width = held_ref.shape[2] // SPLIT
+        for low in range(0, held_ref.shape[2], width):
+            lanes = slice(low, low + width)
+            staged_ref[time, :, lanes] = jnp.dot(
+                chain, held_ref[time, :, lanes], preferred_element_type=jnp.float32
+            ).astype(jnp.bfloat16)
+            copies.append(
+                pltpu.make_async_copy(
+                    staged_ref.at[time, :, lanes], out_ref.at[time, :, lanes], sems.at[len(copies)]
+                )
+            )
+            copies[-1].start()
+
+    write(3, suffix)
+    for k in range(3):
+        write(2 - k, exact_dot(factors_ref[M * k : M * k + M, :], suffix))
+    for copy in copies:
+        copy.wait()
+
+
+SPLIT = 4
+
+
+def smooth(later, factors, held):
+    times = held.shape[0]
     return pl.pallas_call(
         smooth_kernel,
-        grid=(times,),
-        in_specs=[whole, whole, whole, pl.BlockSpec((3 * M, M), lambda t: (0, 0)), block],
-        out_specs=block,
-        out_shape=jax.ShapeDtypeStruct(anomalies.shape, jnp.bfloat16),
-        scratch_shapes=[pltpu.VMEM((4, M, M), jnp.bfloat16)],
+        in_specs=[VMEM] * 5,
+        out_specs=HBM,
+        out_shape=jax.ShapeDtypeStruct(held.shape, held.dtype),
+        scratch_shapes=[pltpu.VMEM(held.shape, held.dtype), pltpu.SemaphoreType.DMA((times * SPLIT,))],
+        compiler_params=pltpu.CompilerParams(vmem_limit_bytes=16 << 20),
         name="smooth",
-    )(*later, factors, anomalies)
+    )(*later, factors, held)
 
 
 XS, ZS, CORES = 4, 8, 2
@@ -286,8 +340,10 @@
 
 def per_device(anomalies, obs_index, obs_weight):
     swap = [(place(*s), place(s[0], s[1], s[2] + 1)) for s in sites()]
-    keep, send = gram_parts(anomalies, obs_index, obs_weight)
-    part = keep + lax.ppermute(send, "space", swap)
+    send, held, index_held, weight_held = gram_other(anomalies, obs_index, obs_weight)
+    received = lax.ppermute(send, "space", swap)
+    keep = gram_own(held, index_held, weight_held)
+    part = keep + received
     around = [
         lax.ppermute(part, "space", [(place(*s), place(s[0] + k, s[1], s[2])) for s in sites()])
         for k in range(1, XS)
@@ -299,8 +355,9 @@
     )
     own = weights_of(parts)
     product, factors = products_of(own, lax.ppermute(own, "space", swap))
-    later = [lax.ppermute(product, "tm", [(g, (g - k) % 4) for g in range(4)]) for k in range(1, 4)]
-    return smooth(later, factors, anomalies)
+    later = [lax.ppermute(product, "tm", [(g, (g - k) % 4) for g in range(4)]) for k in (1, 3, 2)]
+    later = [later[0], later[2], later[1]]
+    return smooth(later, factors, held)
 
 
 def solution(mesh):

time: 72.3 us -> 60.7 us (0.84)
  Pallas kernels: 22 us -> 13.9 us
  waiting for transfers between devices: 10.4 us -> 9.12 us
  local copies, waits for them, and re-layouts: 1.3 us -> 0.04 us
  other arithmetic: 0.92 us -> 0.03 us
    pallas_call x2 -> x3, Pallas kernels: 12.2 us -> 7.35 us  [the longest x1 3.63 us: smooth(): pl.pallas_call(smooth_kernel, in_specs=[VMEM] * 5, out_specs=HBM, out_sha...]
    pallas_call x1, Pallas kernels: 1.95 us -> 0.28 us  [products_of(): pl.pallas_call(products_kernel, out_shape=[jax.ShapeDtypeStruct((M, M), j...]
    pallas_call x1, Pallas kernels: 7.9 us -> 6.23 us  [weights_of(): pl.pallas_call(weights_kernel, out_shape=jax.ShapeDtypeStruct((2 * M, M),...]
    unnamed x8 -> x0, local copies, waits for them, and re-layouts: 1.26 us -> none
    ppermute x1, waiting for transfers between devices: 1.12 us -> 0.01 us  [per_device(): received = lax.ppermute(send, 'space', swap)]
    add x1, other arithmetic: 0.89 us -> 0.01 us  [per_device(): part = keep + received]
  transfers between devices with their start and end apart: 8 -> 8, of which waited for: 7 -> 6; matrix products, arithmetic and copies ran while one was open for 0% -> 0% of each run, Pallas kernels for 0% -> 2%
where the time goes in v2:
time: 60.7 us; the launch traced here: 60.5 us
  blocking collectives  24.1 us (40%)
  Pallas kernels  13.9 us (23%)
  starting transfers between devices  13.2 us (22%)
  waiting for transfers between devices  9.12 us (15%)
    all_to_all x1, blocking collectives, per_device(): lax.all_to_all(jnp.broadcast_to(part[None], (ZS, ROWS, M)), 'space', 0, 0...  24.1 us
    pallas_call x1, Pallas kernels, weights_of(): pl.pallas_call(weights_kernel, out_shape=jax.ShapeDtypeStruct((2 * M, M),...  6.23 us
    ppermute x3, waiting for transfers between devices, per_device(): lax.ppermute(part, 'space', [(place(*s), place(s[0] + k, s[1], s[2])) for...  5.79 us
    ppermute x3, starting transfers between devices, per_device(): lax.ppermute(product, 'tm', [(g, (g - k) % 4) for g in range(4)])  5.05 us
    pallas_call x1, Pallas kernels, smooth(): pl.pallas_call(smooth_kernel, in_specs=[VMEM] * 5, out_specs=HBM, out_sha...  3.63 us
    ppermute x1, starting transfers between devices, per_device(): received = lax.ppermute(send, 'space', swap)  3.29 us
    ppermute x1, starting transfers between devices, per_device(): product, factors = products_of(own, lax.ppermute(own, 'space', swap))  2.91 us
    pallas_call x1, Pallas kernels, gram_other(): pl.pallas_call(gram_other_kernel, in_specs=[HBM] * 3, out_specs=[VMEM] *...  2.7 us
  transfers between devices with their start and end apart: 8, of which 6 were waited for; matrix products, arithmetic and copies ran while one was open for 0% of the time, Pallas kernels for 2%

profile of v2, /device:TPU:1, one launch (start us, length us, event | category | flops | bytes accessed | tf_op | source)
XLA Modules:
  0.0 60.5 jit_solution(16353715364620897687)
XLA Ops:
  0.0 2.7 %gram_other.1 = (f32[136,128]{1,0:T(8,128)S(1)}, bf16[4,128,4096]{2,1,0:T(8,128)(2,1)S(1)}, s32[4,1024]{1,0:T(4,128)S(1)}, f32[4,1024]{1,0:T(4,128)S(1)}) custom-call(bf16[4,128,4096]{2,1,0:T(8,128)(2,1)} %anomalies_ref.1, s32[4,1024]{1,0:T(4,128)} %index_ref.1, f32[4,1024]{1,0:T(4,128)} %weight_ref.1), custom_call_target="tpu_custom_call" | custom-call | flops 268435456 | bytes 2097152 | tf_op jit(solution)/shard_map/gram_other/pallas_call | solution.py:125
  2.7 3.3 %collective-permute-start = (f32[136,128]{1,0:T(8,128)S(1)}, f32[136,128]{1,0:T(8,128)S(1)}, u32[]{:S(2)}, u32[]{:S(2)}) collective-permute-start(f32[136,128]{1,0:T(8,128)S(1)} %get-tuple-element.14), channel_id=1, source_target_pairs={{0,1},{1,0},{2,3},{3,2},{4,5},{5,4},{6,7},{7,6},{8,9},{9,8},{10,11... | collective-permute-start | bytes 208904 | tf_op jit(solution)/shard_map/ppermute | solution.py:344
  6.0 1.0 %gram_own.1 = f32[136,128]{1,0:T(8,128)S(1)} custom-call(bf16[4,128,4096]{2,1,0:T(8,128)(2,1)S(1)} %get-tuple-element.11.held_ref, s32[4,1024]{1,0:T(4,128)S(1)} %get-tuple-element.12.index_ref, f32[4,1024]{1,0:T(4,128)S(1)} %get-tuple-element.13.weight_ref), custom_call_target="tpu_custom_call" | custom-call | flops 268435456 | bytes 2097152 | tf_op jit(solution)/shard_map/gram_own/pallas_call | solution.py:141
  7.0 0.0 collective-permute-done
  7.1 0.8 %collective-permute-start.3 = (f32[136,128]{1,0:T(8,128)S(1)}, f32[136,128]{1,0:T(8,128)S(1)}, u32[]{:S(2)}, u32[]{:S(2)}) collective-permute-start(f32[136,128]{1,0:T(8,128)S(1)} %add.12), channel_id=1, source_target_pairs={{0,48},{1,49},{2,50},{3,51},{4,52},{5,53},{6,54},{7,55},{8,56},{9,... | collective-permute-start | bytes 208904 | tf_op jit(solution)/shard_map/ppermute | solution.py:348
  7.9 0.5 collective-permute-start.2
  8.4 0.6 %collective-permute-start.1 = (f32[136,128]{1,0:T(8,128)S(1)}, f32[136,128]{1,0:T(8,128)S(1)}, u32[]{:S(2)}, u32[]{:S(2)}) collective-permute-start(f32[136,128]{1,0:T(8,128)S(1)} %add.12), channel_id=1, source_target_pairs={{0,16},{1,17},{2,18},{3,19},{4,20},{5,21},{6,22},{7,23},{8,24},{9,... | collective-permute-start | bytes 208904 | tf_op jit(solution)/shard_map/ppermute | solution.py:348
  9.0 1.6 %collective-permute-done.3 = f32[136,128]{1,0:T(8,128)S(1)} collective-permute-done((f32[136,128]{1,0:T(8,128)S(1)}, f32[136,128]{1,0:T(8,128)S(1)}, u32[]{:S(2)}, u32[]{:S(2)}) %collective-permute-start.3) | collective-permute-done | bytes 69664 | tf_op jit(solution)/shard_map/ppermute | solution.py:348
  10.7 2.0 %collective-permute-done.2 = f32[136,128]{1,0:T(8,128)S(1)} collective-permute-done((f32[136,128]{1,0:T(8,128)S(1)}, f32[136,128]{1,0:T(8,128)S(1)}, u32[]{:S(2)}, u32[]{:S(2)}) %collective-permute-start.2) | collective-permute-done | bytes 69664 | tf_op jit(solution)/shard_map/ppermute | solution.py:348
  12.6 2.2 %collective-permute-done.1 = f32[136,128]{1,0:T(8,128)S(1)} collective-permute-done((f32[136,128]{1,0:T(8,128)S(1)}, f32[136,128]{1,0:T(8,128)S(1)}, u32[]{:S(2)}, u32[]{:S(2)}) %collective-permute-start.1) | collective-permute-done | bytes 69664 | tf_op jit(solution)/shard_map/ppermute | solution.py:348
  14.9 24.1 %all_to_all.5.parts_ref = f32[8,136,128]{2,1,0:T(8,128)S(1)} all-to-all(f32[8,136,128]{2,1,0:T(8,128)S(1)} %broadcast_in_dim.2), channel_id=1, replica_groups={{0,2,4,6,8,10,12,14},{1,3,5,7,9,11,13,15},{16,18,20,22,24,26,28,30},{17..., dimensions={0} | all-to-all | bytes 1114112 | tf_op jit(solution)/shard_map/all_to_all | solution.py:353
  39.0 6.2 %weights.1.own_ref = f32[256,128]{1,0:T(8,128)S(1)} custom-call(f32[8,136,128]{2,1,0:T(8,128)S(1)} %all_to_all.5.parts_ref), custom_call_target="tpu_custom_call" | custom-call | tf_op jit(solution)/shard_map/weights/pallas_call | solution.py:253
  45.3 2.9 %collective-permute-start.4 = (f32[256,128]{1,0:T(8,128)S(1)}, f32[256,128]{1,0:T(8,128)S(1)}, u32[]{:S(2)}, u32[]{:S(2)}) collective-permute-start(f32[256,128]{1,0:T(8,128)S(1)} %weights.1.own_ref), channel_id=1, source_target_pairs={{0,1},{1,0},{2,3},{3,2},{4,5},{5,4},{6,7},{7,6},{8,9},{9,8},{10,11... | collective-permute-start | bytes 393224 | tf_op jit(solution)/shard_map/ppermute | solution.py:357
  48.2 1.0 %collective-permute-done.4.other_ref = f32[256,128]{1,0:T(8,128)S(1)} collective-permute-done((f32[256,128]{1,0:T(8,128)S(1)}, f32[256,128]{1,0:T(8,128)S(1)}, u32[]{:S(2)}, u32[]{:S(2)}) %collective-permute-start.4) | collective-permute-done | bytes 131104 | tf_op jit(solution)/shard_map/ppermute | solution.py:357
  49.2 0.3 products.1
  49.5 1.4 %collective-permute-start.7 = (f32[128,128]{1,0:T(8,128)S(1)}, f32[128,128]{1,0:T(8,128)S(1)}, u32[]{:S(2)}, u32[]{:S(2)}) collective-permute-start(f32[128,128]{1,0:T(8,128)S(1)} %get-tuple-element.15), channel_id=1, source_target_pairs={{0,64},{64,128},{128,192},{192,0},{1,65},{65,129},{129,193},{193,1... | collective-permute-start | bytes 196616 | tf_op jit(solution)/shard_map/ppermute | solution.py:358
  50.8 2.6 %collective-permute-start.6 = (f32[128,128]{1,0:T(8,128)S(1)}, f32[128,128]{1,0:T(8,128)S(1)}, u32[]{:S(2)}, u32[]{:S(2)}) collective-permute-start(f32[128,128]{1,0:T(8,128)S(1)} %get-tuple-element.15), channel_id=1, source_target_pairs={{0,128},{64,192},{128,0},{192,64},{1,129},{65,193},{129,1},{193,65... | collective-permute-start | bytes 196616 | tf_op jit(solution)/shard_map/ppermute | solution.py:358
  53.4 1.1 %collective-permute-start.5 = (f32[128,128]{1,0:T(8,128)S(1)}, f32[128,128]{1,0:T(8,128)S(1)}, u32[]{:S(2)}, u32[]{:S(2)}) collective-permute-start(f32[128,128]{1,0:T(8,128)S(1)} %get-tuple-element.15), channel_id=1, source_target_pairs={{0,192},{64,0},{128,64},{192,128},{1,193},{65,1},{129,65},{193,129... | collective-permute-start | bytes 196616 | tf_op jit(solution)/shard_map/ppermute | solution.py:358
  54.5 0.0 collective-permute-done.7.three_ref
  54.5 1.9 %collective-permute-done.6.two_ref = f32[128,128]{1,0:T(8,128)S(1)} collective-permute-done((f32[128,128]{1,0:T(8,128)S(1)}, f32[128,128]{1,0:T(8,128)S(1)}, u32[]{:S(2)}, u32[]{:S(2)}) %collective-permute-start.6) | collective-permute-done | bytes 65568 | tf_op jit(solution)/shard_map/ppermute | solution.py:358
  56.4 0.5 collective-permute-done.5.one_ref
  56.8 3.6 %smooth.1 = bf16[4,128,4096]{2,1,0:T(8,128)(2,1)} custom-call(f32[128,128]{1,0:T(8,128)S(1)} %collective-permute-done.5.one_ref, f32[128,128]{1,0:T(8,128)S(1)} %collective-permute-done.6.two_ref, f32[128,128]{1,0:T(8,128)S(1)} %collective-permute-done.7.three_ref, f32[384,128]{1,0:T(8,128)S(1)} %get-tuple-element.16.factors_ref, ...), custom_call_target="tpu_custom_call" | custom-call | tf_op jit(solution)/shard_map/smooth/pallas_call | solution.py:319
  (3 shorter events, 0.1 us)
Async XLA Ops:
  2.7 4.3 %collective-permute-start = (f32[136,128]{1,0:T(8,128)S(1)}, f32[136,128]{1,0:T(8,128)S(1)}, u32[]{:S(2)}, u32[]{:S(2)}) collective-permute-start(f32[136,128]{1,0:T(8,128)S(1)} %get-tuple-element.14), channel_id=1, source_target_pairs={{0,1},{1,0},{2,3},{3,2},{4,5},{5,4},{6,7},{7,6},{8,9},{9,8},{10,11... | collective-permute-start | bytes 208904 | tf_op jit(solution)/shard_map/ppermute | solution.py:344
  7.1 3.6 %collective-permute-start.3 = (f32[136,128]{1,0:T(8,128)S(1)}, f32[136,128]{1,0:T(8,128)S(1)}, u32[]{:S(2)}, u32[]{:S(2)}) collective-permute-start(f32[136,128]{1,0:T(8,128)S(1)} %add.12), channel_id=1, source_target_pairs={{0,48},{1,49},{2,50},{3,51},{4,52},{5,53},{6,54},{7,55},{8,56},{9,... | collective-permute-start | bytes 208904 | tf_op jit(solution)/shard_map/ppermute | solution.py:348
  7.9 4.7 %collective-permute-start.2 = (f32[136,128]{1,0:T(8,128)S(1)}, f32[136,128]{1,0:T(8,128)S(1)}, u32[]{:S(2)}, u32[]{:S(2)}) collective-permute-start(f32[136,128]{1,0:T(8,128)S(1)} %add.12), channel_id=1, source_target_pairs={{0,32},{1,33},{2,34},{3,35},{4,36},{5,37},{6,38},{7,39},{8,40},{9,... | collective-permute-start | bytes 208904 | tf_op jit(solution)/shard_map/ppermute | solution.py:348
  8.4 6.4 %collective-permute-start.1 = (f32[136,128]{1,0:T(8,128)S(1)}, f32[136,128]{1,0:T(8,128)S(1)}, u32[]{:S(2)}, u32[]{:S(2)}) collective-permute-start(f32[136,128]{1,0:T(8,128)S(1)} %add.12), channel_id=1, source_target_pairs={{0,16},{1,17},{2,18},{3,19},{4,20},{5,21},{6,22},{7,23},{8,24},{9,... | collective-permute-start | bytes 208904 | tf_op jit(solution)/shard_map/ppermute | solution.py:348
  45.3 3.9 %collective-permute-start.4 = (f32[256,128]{1,0:T(8,128)S(1)}, f32[256,128]{1,0:T(8,128)S(1)}, u32[]{:S(2)}, u32[]{:S(2)}) collective-permute-start(f32[256,128]{1,0:T(8,128)S(1)} %weights.1.own_ref), channel_id=1, source_target_pairs={{0,1},{1,0},{2,3},{3,2},{4,5},{5,4},{6,7},{7,6},{8,9},{9,8},{10,11... | collective-permute-start | bytes 393224 | tf_op jit(solution)/shard_map/ppermute | solution.py:357
  49.5 5.1 %collective-permute-start.7 = (f32[128,128]{1,0:T(8,128)S(1)}, f32[128,128]{1,0:T(8,128)S(1)}, u32[]{:S(2)}, u32[]{:S(2)}) collective-permute-start(f32[128,128]{1,0:T(8,128)S(1)} %get-tuple-element.15), channel_id=1, source_target_pairs={{0,64},{64,128},{128,192},{192,0},{1,65},{65,129},{129,193},{193,1... | collective-permute-start | bytes 196616 | tf_op jit(solution)/shard_map/ppermute | solution.py:358
  50.8 5.6 %collective-permute-start.6 = (f32[128,128]{1,0:T(8,128)S(1)}, f32[128,128]{1,0:T(8,128)S(1)}, u32[]{:S(2)}, u32[]{:S(2)}) collective-permute-start(f32[128,128]{1,0:T(8,128)S(1)} %get-tuple-element.15), channel_id=1, source_target_pairs={{0,128},{64,192},{128,0},{192,64},{1,129},{65,193},{129,1},{193,65... | collective-permute-start | bytes 196616 | tf_op jit(solution)/shard_map/ppermute | solution.py:358
  53.4 3.4 %collective-permute-start.5 = (f32[128,128]{1,0:T(8,128)S(1)}, f32[128,128]{1,0:T(8,128)S(1)}, u32[]{:S(2)}, u32[]{:S(2)}) collective-permute-start(f32[128,128]{1,0:T(8,128)S(1)} %get-tuple-element.15), channel_id=1, source_target_pairs={{0,192},{64,0},{128,64},{192,128},{1,193},{65,1},{129,65},{193,129... | collective-permute-start | bytes 196616 | tf_op jit(solution)/shard_map/ppermute | solution.py:358

commit v3 on v2

--- a/solution.py
+++ b/solution.py
@@ -235,11 +235,9 @@
     return inverses
 
 
-def weights_kernel(parts_ref, out_ref):
+def weights_kernel(total_ref, out_ref):
     dof = float(M - 1)
-    total = parts_ref[0]
-    for k in range(1, parts_ref.shape[0]):
-        total = total + parts_ref[k]
+    total = total_ref[...]
     diag = jnp.where(iota((M, M), 0) == iota((M, M), 1), dof, 0.0)
     pair = [
         unfold(total[HALF * k : HALF * k + HALF], total[M + k : M + k + 1]) + diag for k in range(2)
@@ -249,13 +247,13 @@
     out_ref[M:, :] = exact_dot(first, second)
 
 
-def weights_of(parts):
+def weights_of(total):
     return pl.pallas_call(
         weights_kernel,
         out_shape=jax.ShapeDtypeStruct((2 * M, M), jnp.float32),
         compiler_params=pltpu.CompilerParams(vmem_limit_bytes=4 << 20),
         name="weights",
-    )(parts)
+    )(total)
 
 
 def products_kernel(own_ref, other_ref, product_ref, factors_ref):
@@ -344,16 +342,17 @@
     received = lax.ppermute(send, "space", swap)
     keep = gram_own(held, index_held, weight_held)
     part = keep + received
-    around = [
-        lax.ppermute(part, "space", [(place(*s), place(s[0] + k, s[1], s[2])) for s in sites()])
-        for k in range(1, XS)
-    ]
-    part = part + around[0] + around[1] + around[2]
-    groups = [[place(x, z, c) for z in range(ZS)] for x in range(XS) for c in range(CORES)]
-    parts = lax.all_to_all(
-        jnp.broadcast_to(part[None], (ZS, ROWS, M)), "space", 0, 0, axis_index_groups=groups, tiled=True
-    )
-    own = weights_of(parts)
+    for moves in (
+        [lambda x, z: (x, z ^ 1)],
+        [lambda x, z: (x ^ 1, z)],
+        [lambda x, z: (x, z + 2), lambda x, z: (x, z + 6), lambda x, z: (x, z + 4)],
+        [lambda x, z: (x ^ 2, z)],
+    ):
+        part = part + sum(
+            lax.ppermute(part, "space", [(place(x, z, c), place(*move(x, z), c)) for x, z, c in sites()])
+            for move in moves
+        )
+    own = weights_of(part)
     product, factors = products_of(own, lax.ppermute(own, "space", swap))
     later = [lax.ppermute(product, "tm", [(g, (g - k) % 4) for g in range(4)]) for k in (1, 3, 2)]
     later = [later[0], later[2], later[1]]

time: 60.7 us -> 53.5 us (0.88)
  blocking collectives: 24.1 us -> 0 us
  starting transfers between devices: 13.2 us -> 23.3 us
  waiting for transfers between devices: 9.12 us -> 15.5 us
    all_to_all x1 -> x0, blocking collectives: 24.1 us -> none  [per_device(): lax.all_to_all(jnp.broadcast_to(part[None], (ZS, ROWS, M)), 'space', 0, 0...]
    ppermute x3 -> x6, starting transfers between devices: 1.98 us -> 10.7 us  [per_device(): lax.ppermute(part, 'space', [(place(x, z, c), place(*move(x, z), c)) for...]
    ppermute x3 -> x6, waiting for transfers between devices: 5.79 us -> 12.2 us  [per_device(): lax.ppermute(part, 'space', [(place(x, z, c), place(*move(x, z), c)) for...]
    ppermute x1, starting transfers between devices: 2.91 us -> 4.34 us  [per_device(): product, factors = products_of(own, lax.ppermute(own, 'space', swap))]
  transfers between devices with their start and end apart: 8 -> 11, of which waited for: 6 -> 7; matrix products, arithmetic and copies ran while one was open for 0% -> 0% of each run, Pallas kernels for 2% -> 2%
where the time goes in v3:
time: 53.5 us; the launch traced here: 52.8 us
  starting transfers between devices  23.3 us (44%)
  waiting for transfers between devices  15.5 us (29%)
  Pallas kernels  13.9 us (26%)
    ppermute x6, waiting for transfers between devices, per_device(): lax.ppermute(part, 'space', [(place(x, z, c), place(*move(x, z), c)) for...  12.2 us
    ppermute x6, starting transfers between devices, per_device(): lax.ppermute(part, 'space', [(place(x, z, c), place(*move(x, z), c)) for...  10.7 us
    pallas_call x1, Pallas kernels, weights_of(): pl.pallas_call(weights_kernel, out_shape=jax.ShapeDtypeStruct((2 * M, M),...  6.23 us
    ppermute x3, starting transfers between devices, per_device(): lax.ppermute(product, 'tm', [(g, (g - k) % 4) for g in range(4)])  5.06 us
    ppermute x1, starting transfers between devices, per_device(): product, factors = products_of(own, lax.ppermute(own, 'space', swap))  4.34 us
    pallas_call x1, Pallas kernels, smooth(): pl.pallas_call(smooth_kernel, in_specs=[VMEM] * 5, out_specs=HBM, out_sha...  3.63 us
    ppermute x1, starting transfers between devices, per_device(): received = lax.ppermute(send, 'space', swap)  3.29 us
    pallas_call x1, Pallas kernels, gram_other(): pl.pallas_call(gram_other_kernel, in_specs=[HBM] * 3, out_specs=[VMEM] *...  2.7 us
  transfers between devices with their start and end apart: 11, of which 7 were waited for; matrix products, arithmetic and copies ran while one was open for 0% of the time, Pallas kernels for 2%

profile of v3, /device:TPU:1, one launch (start us, length us, event | category | flops | bytes accessed | tf_op | source)
XLA Modules:
  0.0 52.8 jit_solution(12042954820682187735)
XLA Ops:
  0.0 2.7 %gram_other.1 = (f32[136,128]{1,0:T(8,128)S(1)}, bf16[4,128,4096]{2,1,0:T(8,128)(2,1)S(1)}, s32[4,1024]{1,0:T(4,128)S(1)}, f32[4,1024]{1,0:T(4,128)S(1)}) custom-call(bf16[4,128,4096]{2,1,0:T(8,128)(2,1)} %anomalies_ref.1, s32[4,1024]{1,0:T(4,128)} %index_ref.1, f32[4,1024]{1,0:T(4,128)} %weight_ref.1), custom_call_target="tpu_custom_call" | custom-call | flops 268435456 | bytes 2097152 | tf_op jit(solution)/shard_map/gram_other/pallas_call | solution.py:125
  2.7 3.3 %collective-permute-start = (f32[136,128]{1,0:T(8,128)S(1)}, f32[136,128]{1,0:T(8,128)S(1)}, u32[]{:S(2)}, u32[]{:S(2)}) collective-permute-start(f32[136,128]{1,0:T(8,128)S(1)} %get-tuple-element.14), channel_id=1, source_target_pairs={{0,1},{1,0},{2,3},{3,2},{4,5},{5,4},{6,7},{7,6},{8,9},{9,8},{10,11... | collective-permute-start | bytes 208904 | tf_op jit(solution)/shard_map/ppermute | solution.py:342
  6.0 1.0 %gram_own.1 = f32[136,128]{1,0:T(8,128)S(1)} custom-call(bf16[4,128,4096]{2,1,0:T(8,128)(2,1)S(1)} %get-tuple-element.11.held_ref, s32[4,1024]{1,0:T(4,128)S(1)} %get-tuple-element.12.index_ref, f32[4,1024]{1,0:T(4,128)S(1)} %get-tuple-element.13.weight_ref), custom_call_target="tpu_custom_call" | custom-call | flops 268435456 | bytes 2097152 | tf_op jit(solution)/shard_map/gram_own/pallas_call | solution.py:141
  7.0 0.0 collective-permute-done
  7.1 0.1 collective-permute-start.1
  7.2 3.5 %collective-permute-done.1 = f32[136,128]{1,0:T(8,128)S(1)} collective-permute-done((f32[136,128]{1,0:T(8,128)S(1)}, f32[136,128]{1,0:T(8,128)S(1)}, u32[]{:S(2)}, u32[]{:S(2)}) %collective-permute-start.1) | collective-permute-done | bytes 69664 | tf_op jit(solution)/shard_map/ppermute | solution.py:352
  10.7 0.1 collective-permute-start.2
  10.8 3.1 %collective-permute-done.2 = f32[136,128]{1,0:T(8,128)S(1)} collective-permute-done((f32[136,128]{1,0:T(8,128)S(1)}, f32[136,128]{1,0:T(8,128)S(1)}, u32[]{:S(2)}, u32[]{:S(2)}) %collective-permute-start.2) | collective-permute-done | bytes 69664 | tf_op jit(solution)/shard_map/ppermute | solution.py:352
  14.0 5.3 %collective-permute-start.5 = (f32[136,128]{1,0:T(8,128)S(1)}, f32[136,128]{1,0:T(8,128)S(1)}, u32[]{:S(2)}, u32[]{:S(2)}) collective-permute-start(f32[136,128]{1,0:T(8,128)S(1)} %add.23), channel_id=1, source_target_pairs={{0,8},{1,9},{2,10},{3,11},{4,12},{5,13},{6,14},{7,15},{8,0},{9,1},... | collective-permute-start | bytes 208904 | tf_op jit(solution)/shard_map/ppermute | solution.py:352
  19.2 0.0 collective-permute-start.4
  19.2 2.4 %collective-permute-start.3 = (f32[136,128]{1,0:T(8,128)S(1)}, f32[136,128]{1,0:T(8,128)S(1)}, u32[]{:S(2)}, u32[]{:S(2)}) collective-permute-start(f32[136,128]{1,0:T(8,128)S(1)} %add.23), channel_id=1, source_target_pairs={{0,4},{1,5},{2,6},{3,7},{4,8},{5,9},{6,10},{7,11},{8,12},{9,13},{1... | collective-permute-start | bytes 208904 | tf_op jit(solution)/shard_map/ppermute | solution.py:352
  21.6 0.0 collective-permute-done.5
  21.6 3.6 %collective-permute-done.4 = f32[136,128]{1,0:T(8,128)S(1)} collective-permute-done((f32[136,128]{1,0:T(8,128)S(1)}, f32[136,128]{1,0:T(8,128)S(1)}, u32[]{:S(2)}, u32[]{:S(2)}) %collective-permute-start.4) | collective-permute-done | bytes 69664 | tf_op jit(solution)/shard_map/ppermute | solution.py:352
  25.2 0.0 collective-permute-done.3
  25.2 2.8 %collective-permute-start.6 = (f32[136,128]{1,0:T(8,128)S(1)}, f32[136,128]{1,0:T(8,128)S(1)}, u32[]{:S(2)}, u32[]{:S(2)}) collective-permute-start(f32[136,128]{1,0:T(8,128)S(1)} %add_add_fusion), channel_id=1, source_target_pairs={{0,32},{1,33},{2,34},{3,35},{4,36},{5,37},{6,38},{7,39},{8,40},{9,... | collective-permute-start | bytes 208904 | tf_op jit(solution)/shard_map/ppermute | solution.py:352
  28.0 1.9 %collective-permute-done.6 = f32[136,128]{1,0:T(8,128)S(1)} collective-permute-done((f32[136,128]{1,0:T(8,128)S(1)}, f32[136,128]{1,0:T(8,128)S(1)}, u32[]{:S(2)}, u32[]{:S(2)}) %collective-permute-start.6) | collective-permute-done | bytes 69664 | tf_op jit(solution)/shard_map/ppermute | solution.py:352
  30.0 6.2 %weights.1.own_ref = f32[256,128]{1,0:T(8,128)S(1)} custom-call(f32[136,128]{1,0:T(8,128)S(1)} %add.27.total_ref), custom_call_target="tpu_custom_call" | custom-call | tf_op jit(solution)/shard_map/weights/pallas_call | solution.py:251
  36.2 4.3 %collective-permute-start.7 = (f32[256,128]{1,0:T(8,128)S(1)}, f32[256,128]{1,0:T(8,128)S(1)}, u32[]{:S(2)}, u32[]{:S(2)}) collective-permute-start(f32[256,128]{1,0:T(8,128)S(1)} %weights.1.own_ref), channel_id=1, source_target_pairs={{0,1},{1,0},{2,3},{3,2},{4,5},{5,4},{6,7},{7,6},{8,9},{9,8},{10,11... | collective-permute-start | bytes 393224 | tf_op jit(solution)/shard_map/ppermute | solution.py:356
  40.5 1.0 %collective-permute-done.7.other_ref = f32[256,128]{1,0:T(8,128)S(1)} collective-permute-done((f32[256,128]{1,0:T(8,128)S(1)}, f32[256,128]{1,0:T(8,128)S(1)}, u32[]{:S(2)}, u32[]{:S(2)}) %collective-permute-start.7) | collective-permute-done | bytes 131104 | tf_op jit(solution)/shard_map/ppermute | solution.py:356
  41.5 0.3 products.1
  41.8 1.4 %collective-permute-start.10 = (f32[128,128]{1,0:T(8,128)S(1)}, f32[128,128]{1,0:T(8,128)S(1)}, u32[]{:S(2)}, u32[]{:S(2)}) collective-permute-start(f32[128,128]{1,0:T(8,128)S(1)} %get-tuple-element.15), channel_id=1, source_target_pairs={{0,64},{64,128},{128,192},{192,0},{1,65},{65,129},{129,193},{193,1... | collective-permute-start | bytes 196616 | tf_op jit(solution)/shard_map/ppermute | solution.py:357
  43.2 2.6 %collective-permute-start.9 = (f32[128,128]{1,0:T(8,128)S(1)}, f32[128,128]{1,0:T(8,128)S(1)}, u32[]{:S(2)}, u32[]{:S(2)}) collective-permute-start(f32[128,128]{1,0:T(8,128)S(1)} %get-tuple-element.15), channel_id=1, source_target_pairs={{0,128},{64,192},{128,0},{192,64},{1,129},{65,193},{129,1},{193,65... | collective-permute-start | bytes 196616 | tf_op jit(solution)/shard_map/ppermute | solution.py:357
  45.8 1.1 %collective-permute-start.8 = (f32[128,128]{1,0:T(8,128)S(1)}, f32[128,128]{1,0:T(8,128)S(1)}, u32[]{:S(2)}, u32[]{:S(2)}) collective-permute-start(f32[128,128]{1,0:T(8,128)S(1)} %get-tuple-element.15), channel_id=1, source_target_pairs={{0,192},{64,0},{128,64},{192,128},{1,193},{65,1},{129,65},{193,129... | collective-permute-start | bytes 196616 | tf_op jit(solution)/shard_map/ppermute | solution.py:357
  46.9 0.0 collective-permute-done.10.three_ref
  46.9 1.9 %collective-permute-done.9.two_ref = f32[128,128]{1,0:T(8,128)S(1)} collective-permute-done((f32[128,128]{1,0:T(8,128)S(1)}, f32[128,128]{1,0:T(8,128)S(1)}, u32[]{:S(2)}, u32[]{:S(2)}) %collective-permute-start.9) | collective-permute-done | bytes 65568 | tf_op jit(solution)/shard_map/ppermute | solution.py:357
  48.7 0.5 collective-permute-done.8.one_ref
  49.2 3.6 %smooth.1 = bf16[4,128,4096]{2,1,0:T(8,128)(2,1)} custom-call(f32[128,128]{1,0:T(8,128)S(1)} %collective-permute-done.8.one_ref, f32[128,128]{1,0:T(8,128)S(1)} %collective-permute-done.9.two_ref, f32[128,128]{1,0:T(8,128)S(1)} %collective-permute-done.10.three_ref, f32[384,128]{1,0:T(8,128)S(1)} %get-tuple-element.16.factors_ref, ...), custom_call_target="tpu_custom_call" | custom-call | tf_op jit(solution)/shard_map/smooth/pallas_call | solution.py:317
  (5 shorter events, 0.1 us)
Async XLA Ops:
  2.7 4.3 %collective-permute-start = (f32[136,128]{1,0:T(8,128)S(1)}, f32[136,128]{1,0:T(8,128)S(1)}, u32[]{:S(2)}, u32[]{:S(2)}) collective-permute-start(f32[136,128]{1,0:T(8,128)S(1)} %get-tuple-element.14), channel_id=1, source_target_pairs={{0,1},{1,0},{2,3},{3,2},{4,5},{5,4},{6,7},{7,6},{8,9},{9,8},{10,11... | collective-permute-start | bytes 208904 | tf_op jit(solution)/shard_map/ppermute | solution.py:342
  7.1 3.6 %collective-permute-start.1 = (f32[136,128]{1,0:T(8,128)S(1)}, f32[136,128]{1,0:T(8,128)S(1)}, u32[]{:S(2)}, u32[]{:S(2)}) collective-permute-start(f32[136,128]{1,0:T(8,128)S(1)} %add.21), channel_id=1, source_target_pairs={{0,2},{1,3},{2,0},{3,1},{4,6},{5,7},{6,4},{7,5},{8,10},{9,11},{10,... | collective-permute-start | bytes 208904 | tf_op jit(solution)/shard_map/ppermute | solution.py:352
  10.7 3.2 %collective-permute-start.2 = (f32[136,128]{1,0:T(8,128)S(1)}, f32[136,128]{1,0:T(8,128)S(1)}, u32[]{:S(2)}, u32[]{:S(2)}) collective-permute-start(f32[136,128]{1,0:T(8,128)S(1)} %add.22), channel_id=1, source_target_pairs={{0,16},{1,17},{2,18},{3,19},{4,20},{5,21},{6,22},{7,23},{8,24},{9,... | collective-permute-start | bytes 208904 | tf_op jit(solution)/shard_map/ppermute | solution.py:352
  14.0 7.7 %collective-permute-start.5 = (f32[136,128]{1,0:T(8,128)S(1)}, f32[136,128]{1,0:T(8,128)S(1)}, u32[]{:S(2)}, u32[]{:S(2)}) collective-permute-start(f32[136,128]{1,0:T(8,128)S(1)} %add.23), channel_id=1, source_target_pairs={{0,8},{1,9},{2,10},{3,11},{4,12},{5,13},{6,14},{7,15},{8,0},{9,1},... | collective-permute-start | bytes 208904 | tf_op jit(solution)/shard_map/ppermute | solution.py:352
  19.2 5.9 %collective-permute-start.4 = (f32[136,128]{1,0:T(8,128)S(1)}, f32[136,128]{1,0:T(8,128)S(1)}, u32[]{:S(2)}, u32[]{:S(2)}) collective-permute-start(f32[136,128]{1,0:T(8,128)S(1)} %add.23), channel_id=1, source_target_pairs={{0,12},{1,13},{2,14},{3,15},{4,0},{5,1},{6,2},{7,3},{8,4},{9,5},{1... | collective-permute-start | bytes 208904 | tf_op jit(solution)/shard_map/ppermute | solution.py:352
  19.2 5.9 %collective-permute-start.3 = (f32[136,128]{1,0:T(8,128)S(1)}, f32[136,128]{1,0:T(8,128)S(1)}, u32[]{:S(2)}, u32[]{:S(2)}) collective-permute-start(f32[136,128]{1,0:T(8,128)S(1)} %add.23), channel_id=1, source_target_pairs={{0,4},{1,5},{2,6},{3,7},{4,8},{5,9},{6,10},{7,11},{8,12},{9,13},{1... | collective-permute-start | bytes 208904 | tf_op jit(solution)/shard_map/ppermute | solution.py:352
  25.2 4.8 %collective-permute-start.6 = (f32[136,128]{1,0:T(8,128)S(1)}, f32[136,128]{1,0:T(8,128)S(1)}, u32[]{:S(2)}, u32[]{:S(2)}) collective-permute-start(f32[136,128]{1,0:T(8,128)S(1)} %add_add_fusion), channel_id=1, source_target_pairs={{0,32},{1,33},{2,34},{3,35},{4,36},{5,37},{6,38},{7,39},{8,40},{9,... | collective-permute-start | bytes 208904 | tf_op jit(solution)/shard_map/ppermute | solution.py:352
  36.2 5.3 %collective-permute-start.7 = (f32[256,128]{1,0:T(8,128)S(1)}, f32[256,128]{1,0:T(8,128)S(1)}, u32[]{:S(2)}, u32[]{:S(2)}) collective-permute-start(f32[256,128]{1,0:T(8,128)S(1)} %weights.1.own_ref), channel_id=1, source_target_pairs={{0,1},{1,0},{2,3},{3,2},{4,5},{5,4},{6,7},{7,6},{8,9},{9,8},{10,11... | collective-permute-start | bytes 393224 | tf_op jit(solution)/shard_map/ppermute | solution.py:356
  41.8 5.1 %collective-permute-start.10 = (f32[128,128]{1,0:T(8,128)S(1)}, f32[128,128]{1,0:T(8,128)S(1)}, u32[]{:S(2)}, u32[]{:S(2)}) collective-permute-start(f32[128,128]{1,0:T(8,128)S(1)} %get-tuple-element.15), channel_id=1, source_target_pairs={{0,64},{64,128},{128,192},{192,0},{1,65},{65,129},{129,193},{193,1... | collective-permute-start | bytes 196616 | tf_op jit(solution)/shard_map/ppermute | solution.py:357
  43.2 5.5 %collective-permute-start.9 = (f32[128,128]{1,0:T(8,128)S(1)}, f32[128,128]{1,0:T(8,128)S(1)}, u32[]{:S(2)}, u32[]{:S(2)}) collective-permute-start(f32[128,128]{1,0:T(8,128)S(1)} %get-tuple-element.15), channel_id=1, source_target_pairs={{0,128},{64,192},{128,0},{192,64},{1,129},{65,193},{129,1},{193,65... | collective-permute-start | bytes 196616 | tf_op jit(solution)/shard_map/ppermute | solution.py:357
  45.8 3.4 %collective-permute-start.8 = (f32[128,128]{1,0:T(8,128)S(1)}, f32[128,128]{1,0:T(8,128)S(1)}, u32[]{:S(2)}, u32[]{:S(2)}) collective-permute-start(f32[128,128]{1,0:T(8,128)S(1)} %get-tuple-element.15), channel_id=1, source_target_pairs={{0,192},{64,0},{128,64},{192,128},{1,193},{65,1},{129,65},{193,129... | collective-permute-start | bytes 196616 | tf_op jit(solution)/shard_map/ppermute | solution.py:357

commit v4 on v3

--- a/solution.py
+++ b/solution.py
@@ -149,6 +149,35 @@
     )(held, obs_index, obs_weight)
 
 
+def invert_four(at):
+    e11, e12, e22 = at(0, 0), at(0, 1), at(1, 1)
+    f11, f12, f21, f22 = at(0, 2), at(0, 3), at(1, 2), at(1, 3)
+    h11, h12, h22 = at(2, 2), at(2, 3), at(3, 3)
+    d = 1.0 / (e11 * e22 - e12 * e12)
+    x11, x12 = (e22 * f11 - e12 * f21) * d, (e22 * f12 - e12 * f22) * d
+    x21, x22 = (e11 * f21 - e12 * f11) * d, (e11 * f22 - e12 * f12) * d
+    s11 = h11 - (f11 * x11 + f21 * x21)
+    s12 = h12 - (f11 * x12 + f21 * x22)
+    s22 = h22 - (f12 * x12 + f22 * x22)
+    g = 1.0 / (s11 * s22 - s12 * s12)
+    m33, m34, m44 = s22 * g, -s12 * g, s11 * g
+    m13, m14 = -(x11 * m33 + x12 * m34), -(x11 * m34 + x12 * m44)
+    m23, m24 = -(x21 * m33 + x22 * m34), -(x21 * m34 + x22 * m44)
+    m11 = e22 * d - (m13 * x11 + m14 * x12)
+    m12 = -e12 * d - (m13 * x21 + m14 * x22)
+    m22 = e11 * d - (m23 * x21 + m24 * x22)
+    return (
+        (m11, m12, m13, m14),
+        (m12, m22, m23, m24),
+        (m13, m23, m33, m34),
+        (m14, m24, m34, m44),
+    )
+
+
+def weighted(line, values):
+    return (line[0] * values[0] + line[1] * values[1]) + (line[2] * values[2] + line[3] * values[3])
+
+
 def invert_halves(panels):
     lane = iota((8, LANES), 1)
     column = jnp.bitwise_and(lane, HALF - 1)
@@ -161,54 +190,43 @@
     def row_of(panel, k):
         return jnp.broadcast_to(panel[k : k + 1, :], panel.shape)
 
-    for start in range(0, HALF, 4):
-        own, offset = start // 8, start % 8
-        rows = [row_of(panels[own], offset + j) for j in range(4)]
-        columns = [column_of(panels[own], start + j) for j in range(4)]
-
-        def at(i, j):
-            return row_of(columns[j], offset + i)
-
-        e11, e12, e22 = at(0, 0), at(0, 1), at(1, 1)
-        f11, f12, f21, f22 = at(0, 2), at(0, 3), at(1, 2), at(1, 3)
-        h11, h12, h22 = at(2, 2), at(2, 3), at(3, 3)
-        d = 1.0 / (e11 * e22 - e12 * e12)
-        x11, x12 = (e22 * f11 - e12 * f21) * d, (e22 * f12 - e12 * f22) * d
-        x21, x22 = (e11 * f21 - e12 * f11) * d, (e11 * f22 - e12 * f12) * d
-        s11 = h11 - (f11 * x11 + f21 * x21)
-        s12 = h12 - (f11 * x12 + f21 * x22)
-        s22 = h22 - (f12 * x12 + f22 * x22)
-        g = 1.0 / (s11 * s22 - s12 * s12)
-        m33, m34, m44 = s22 * g, -s12 * g, s11 * g
-        m13, m14 = -(x11 * m33 + x12 * m34), -(x11 * m34 + x12 * m44)
-        m23, m24 = -(x21 * m33 + x22 * m34), -(x21 * m34 + x22 * m44)
-        m11 = e22 * d - (m13 * x11 + m14 * x12)
-        m12 = -e12 * d - (m13 * x21 + m14 * x22)
-        m22 = e11 * d - (m23 * x21 + m24 * x22)
-        inverse = (
-            (m11, m12, m13, m14),
-            (m12, m22, m23, m24),
-            (m13, m23, m33, m34),
-            (m14, m24, m34, m44),
-        )
+    def solve(panel, start, offset, inverse):
         pivots = (column >= start) & (column < start + 4)
-        rows = [jnp.where(pivots, jnp.where(column == start + j, 1.0, 0.0), rows[j]) for j in range(4)]
-        solved = [
-            (line[0] * rows[0] + line[1] * rows[1]) + (line[2] * rows[2] + line[3] * rows[3]) for line in inverse
+        rows = [
+            jnp.where(pivots, jnp.where(column == start + j, 1.0, 0.0), row_of(panel, offset + j)) for j in range(4)
         ]
+        return pivots, [weighted(line, rows) for line in inverse]
+
+    def eliminate(panel, pivots, columns, solved):
+        out = jnp.where(pivots, 0.0, panel)
+        return out - weighted(columns, solved)
+
+    def place_rows(panel, offset, solved):
+        for i in range(4):
+            panel = jnp.where(row == offset + i, solved[i], panel)
+        return panel
+
+    count = len(panels)
+    for own in range(count):
+        start = 8 * own
+        columns = [column_of(panels[own], start + k) for k in range(8)]
+        inverse = invert_four(lambda i, j: row_of(columns[j], i))
+        pivots, solved = solve(panels[own], start, 0, inverse)
+        ahead = [
+            [weighted(line, [row_of(columns[k], l) for l in range(4)]) for line in inverse] for k in range(4, 8)
+        ]
+        later = [columns[4 + k] - weighted(columns[:4], ahead[k]) for k in range(4)]
+        second = invert_four(lambda i, j: row_of(later[j], 4 + i))
+        current = place_rows(eliminate(panels[own], pivots, columns[:4], solved), 0, solved)
+        pivots_two, solved_two = solve(current, start + 4, 4, second)
         result = list(panels)
-        order = [(own + (start % 8 == 4) + q) % 8 for q in range(8)]
-        spread = [
-            {p: columns[j] if p == own else column_of(panels[p], start + j) for p in order} for j in range(4)
-        ]
-        for p in order:
-            out = jnp.where(pivots, 0.0, panels[p])
-            for j in range(4):
-                out = out - spread[j][p] * solved[j]
-            if p == own:
-                for i in range(4):
-                    out = jnp.where(row == offset + i, solved[i], out)
-            result[p] = out
+        for p in [(own + 1 + q) % count for q in range(count - 1)]:
+            near = [column_of(panels[p], start + j) for j in range(4)]
+            far = [column_of(panels[p], start + 4 + k) - weighted(near, ahead[k]) for k in range(4)]
+            out = eliminate(panels[p], pivots, near, solved)
+            result[p] = eliminate(out, pivots_two, far, solved_two)
+        far = [column_of(current, start + 4 + k) for k in range(4)]
+        result[own] = place_rows(eliminate(current, pivots_two, far, solved_two), 4, solved_two)
         panels = result
     return panels
 
@@ -225,6 +243,9 @@
     firsts = (first, pltpu.roll(first, HALF, 1))
     crosses = [exact_dot(g[HALF:, :HALF], f[:, :HALF]) for g, f in zip(pair, firsts)]
     schur = [g[HALF:] - exact_dot(x, g[:HALF]) for g, x in zip(pair, crosses)]
+    changes = [exact_dot(s[:, :HALF], f[:, :HALF]) for s, f in zip(schur, firsts)]
+    schur = [s - exact_dot(x, g[:HALF]) for s, x, g in zip(schur, changes, pair)]
+    crosses = [x + change for x, change in zip(crosses, changes)]
     second = invert_packed(jnp.where(left, pltpu.roll(schur[0], HALF, 1), schur[1]))
     seconds = (second, pltpu.roll(second, HALF, 1))
     inverses = []
@@ -284,11 +305,11 @@
     later = [
         jnp.where(position + k < 4, ref[...], eye) for k, ref in ((1, one_ref), (2, two_ref), (3, three_ref))
     ]
-    suffix = exact_dot(later[0], exact_dot(later[1], later[2]))
+    suffix = exact_dot(later[0], exact_dot(later[1], later[2])).T
     copies = []
 
     def write(time, chain):
-        chain = chain.T.astype(jnp.bfloat16)
+        chain = chain.astype(jnp.bfloat16)
         width = held_ref.shape[2] // SPLIT
         for low in range(0, held_ref.shape[2], width):
             lanes = slice(low, low + width)
@@ -304,7 +325,7 @@
 
     write(3, suffix)
     for k in range(3):
-        write(2 - k, exact_dot(factors_ref[M * k : M * k + M, :], suffix))
+        write(2 - k, exact_dot(suffix, factors_ref[M * k : M * k + M, :], NT))
     for copy in copies:
         copy.wait()
 
@@ -343,8 +364,8 @@
     keep = gram_own(held, index_held, weight_held)
     part = keep + received
     for moves in (
+        [lambda x, z: (x ^ 1, z)],
         [lambda x, z: (x, z ^ 1)],
-        [lambda x, z: (x ^ 1, z)],
         [lambda x, z: (x, z + 2), lambda x, z: (x, z + 6), lambda x, z: (x, z + 4)],
         [lambda x, z: (x ^ 2, z)],
     ):
@@ -354,8 +375,8 @@
         )
     own = weights_of(part)
     product, factors = products_of(own, lax.ppermute(own, "space", swap))
-    later = [lax.ppermute(product, "tm", [(g, (g - k) % 4) for g in range(4)]) for k in (1, 3, 2)]
-    later = [later[0], later[2], later[1]]
+    later = [lax.ppermute(product, "tm", [(g, (g - k) % 4) for g in range(4)]) for k in (3, 2, 1)]
+    later = [later[2], later[1], later[0]]
     return smooth(later, factors, held)
 
 

time: 53.5 us -> 53 us (level)
  Pallas kernels: 13.9 us -> 13.3 us
    pallas_call x1, Pallas kernels: 6.23 us -> 5.67 us  [weights_of(): pl.pallas_call(weights_kernel, out_shape=jax.ShapeDtypeStruct((2 * M, M),...]
where the time goes in v4:
time: 53 us; the launch traced here: 52.4 us
  starting transfers between devices  23.3 us (44%)
  waiting for transfers between devices  15.5 us (29%)
  Pallas kernels  13.3 us (25%)
    ppermute x6, waiting for transfers between devices, per_device(): lax.ppermute(part, 'space', [(place(x, z, c), place(*move(x, z), c)) for...  12.2 us
    ppermute x6, starting transfers between devices, per_device(): lax.ppermute(part, 'space', [(place(x, z, c), place(*move(x, z), c)) for...  10.7 us
    pallas_call x1, Pallas kernels, weights_of(): pl.pallas_call(weights_kernel, out_shape=jax.ShapeDtypeStruct((2 * M, M),...  5.67 us
    ppermute x3, starting transfers between devices, per_device(): lax.ppermute(product, 'tm', [(g, (g - k) % 4) for g in range(4)])  5.07 us
    ppermute x1, starting transfers between devices, per_device(): product, factors = products_of(own, lax.ppermute(own, 'space', swap))  4.28 us
    pallas_call x1, Pallas kernels, smooth(): pl.pallas_call(smooth_kernel, in_specs=[VMEM] * 5, out_specs=HBM, out_sha...  3.6 us
    ppermute x1, starting transfers between devices, per_device(): received = lax.ppermute(send, 'space', swap)  3.29 us
    pallas_call x1, Pallas kernels, gram_other(): pl.pallas_call(gram_other_kernel, in_specs=[HBM] * 3, out_specs=[VMEM] *...  2.7 us
  transfers between devices with their start and end apart: 11, of which 7 were waited for; matrix products, arithmetic and copies ran while one was open for 0% of the time, Pallas kernels for 2%

profile of v4, /device:TPU:1, one launch (start us, length us, event | category | flops | bytes accessed | tf_op | source)
XLA Modules:
  0.0 52.4 jit_solution(3819893678696922019)
XLA Ops:
  0.0 2.7 %gram_other.1 = (f32[136,128]{1,0:T(8,128)S(1)}, bf16[4,128,4096]{2,1,0:T(8,128)(2,1)S(1)}, s32[4,1024]{1,0:T(4,128)S(1)}, f32[4,1024]{1,0:T(4,128)S(1)}) custom-call(bf16[4,128,4096]{2,1,0:T(8,128)(2,1)} %anomalies_ref.1, s32[4,1024]{1,0:T(4,128)} %index_ref.1, f32[4,1024]{1,0:T(4,128)} %weight_ref.1), custom_call_target="tpu_custom_call" | custom-call | flops 268435456 | bytes 2097152 | tf_op jit(solution)/shard_map/gram_other/pallas_call | solution.py:125
  2.7 3.3 %collective-permute-start = (f32[136,128]{1,0:T(8,128)S(1)}, f32[136,128]{1,0:T(8,128)S(1)}, u32[]{:S(2)}, u32[]{:S(2)}) collective-permute-start(f32[136,128]{1,0:T(8,128)S(1)} %get-tuple-element.14), channel_id=1, source_target_pairs={{0,1},{1,0},{2,3},{3,2},{4,5},{5,4},{6,7},{7,6},{8,9},{9,8},{10,11... | collective-permute-start | bytes 208904 | tf_op jit(solution)/shard_map/ppermute | solution.py:363
  6.0 1.0 %gram_own.1 = f32[136,128]{1,0:T(8,128)S(1)} custom-call(bf16[4,128,4096]{2,1,0:T(8,128)(2,1)S(1)} %get-tuple-element.11.held_ref, s32[4,1024]{1,0:T(4,128)S(1)} %get-tuple-element.12.index_ref, f32[4,1024]{1,0:T(4,128)S(1)} %get-tuple-element.13.weight_ref), custom_call_target="tpu_custom_call" | custom-call | flops 268435456 | bytes 2097152 | tf_op jit(solution)/shard_map/gram_own/pallas_call | solution.py:141
  7.0 0.0 collective-permute-done
  7.1 0.1 collective-permute-start.1
  7.2 3.5 %collective-permute-done.1 = f32[136,128]{1,0:T(8,128)S(1)} collective-permute-done((f32[136,128]{1,0:T(8,128)S(1)}, f32[136,128]{1,0:T(8,128)S(1)}, u32[]{:S(2)}, u32[]{:S(2)}) %collective-permute-start.1) | collective-permute-done | bytes 69664 | tf_op jit(solution)/shard_map/ppermute | solution.py:373
  10.7 0.1 collective-permute-start.2
  10.8 3.1 %collective-permute-done.2 = f32[136,128]{1,0:T(8,128)S(1)} collective-permute-done((f32[136,128]{1,0:T(8,128)S(1)}, f32[136,128]{1,0:T(8,128)S(1)}, u32[]{:S(2)}, u32[]{:S(2)}) %collective-permute-start.2) | collective-permute-done | bytes 69664 | tf_op jit(solution)/shard_map/ppermute | solution.py:373
  13.9 5.3 %collective-permute-start.5 = (f32[136,128]{1,0:T(8,128)S(1)}, f32[136,128]{1,0:T(8,128)S(1)}, u32[]{:S(2)}, u32[]{:S(2)}) collective-permute-start(f32[136,128]{1,0:T(8,128)S(1)} %add.23), channel_id=1, source_target_pairs={{0,8},{1,9},{2,10},{3,11},{4,12},{5,13},{6,14},{7,15},{8,0},{9,1},... | collective-permute-start | bytes 208904 | tf_op jit(solution)/shard_map/ppermute | solution.py:373
  19.2 0.0 collective-permute-start.4
  19.2 2.4 %collective-permute-start.3 = (f32[136,128]{1,0:T(8,128)S(1)}, f32[136,128]{1,0:T(8,128)S(1)}, u32[]{:S(2)}, u32[]{:S(2)}) collective-permute-start(f32[136,128]{1,0:T(8,128)S(1)} %add.23), channel_id=1, source_target_pairs={{0,4},{1,5},{2,6},{3,7},{4,8},{5,9},{6,10},{7,11},{8,12},{9,13},{1... | collective-permute-start | bytes 208904 | tf_op jit(solution)/shard_map/ppermute | solution.py:373
  21.6 0.0 collective-permute-done.5
  21.6 3.6 %collective-permute-done.4 = f32[136,128]{1,0:T(8,128)S(1)} collective-permute-done((f32[136,128]{1,0:T(8,128)S(1)}, f32[136,128]{1,0:T(8,128)S(1)}, u32[]{:S(2)}, u32[]{:S(2)}) %collective-permute-start.4) | collective-permute-done | bytes 69664 | tf_op jit(solution)/shard_map/ppermute | solution.py:373
  25.2 0.0 collective-permute-done.3
  25.2 2.8 %collective-permute-start.6 = (f32[136,128]{1,0:T(8,128)S(1)}, f32[136,128]{1,0:T(8,128)S(1)}, u32[]{:S(2)}, u32[]{:S(2)}) collective-permute-start(f32[136,128]{1,0:T(8,128)S(1)} %add_add_fusion), channel_id=1, source_target_pairs={{0,32},{1,33},{2,34},{3,35},{4,36},{5,37},{6,38},{7,39},{8,40},{9,... | collective-permute-start | bytes 208904 | tf_op jit(solution)/shard_map/ppermute | solution.py:373
  28.0 1.9 %collective-permute-done.6 = f32[136,128]{1,0:T(8,128)S(1)} collective-permute-done((f32[136,128]{1,0:T(8,128)S(1)}, f32[136,128]{1,0:T(8,128)S(1)}, u32[]{:S(2)}, u32[]{:S(2)}) %collective-permute-start.6) | collective-permute-done | bytes 69664 | tf_op jit(solution)/shard_map/ppermute | solution.py:373
  30.0 5.7 %weights.1.own_ref = f32[256,128]{1,0:T(8,128)S(1)} custom-call(f32[136,128]{1,0:T(8,128)S(1)} %add.27.total_ref), custom_call_target="tpu_custom_call" | custom-call | tf_op jit(solution)/shard_map/weights/pallas_call | solution.py:272
  35.6 4.3 %collective-permute-start.7 = (f32[256,128]{1,0:T(8,128)S(1)}, f32[256,128]{1,0:T(8,128)S(1)}, u32[]{:S(2)}, u32[]{:S(2)}) collective-permute-start(f32[256,128]{1,0:T(8,128)S(1)} %weights.1.own_ref), channel_id=1, source_target_pairs={{0,1},{1,0},{2,3},{3,2},{4,5},{5,4},{6,7},{7,6},{8,9},{9,8},{10,11... | collective-permute-start | bytes 393224 | tf_op jit(solution)/shard_map/ppermute | solution.py:377
  39.9 1.0 %collective-permute-done.7.other_ref = f32[256,128]{1,0:T(8,128)S(1)} collective-permute-done((f32[256,128]{1,0:T(8,128)S(1)}, f32[256,128]{1,0:T(8,128)S(1)}, u32[]{:S(2)}, u32[]{:S(2)}) %collective-permute-start.7) | collective-permute-done | bytes 131104 | tf_op jit(solution)/shard_map/ppermute | solution.py:377
  40.9 0.3 products.1
  41.2 1.4 %collective-permute-start.10 = (f32[128,128]{1,0:T(8,128)S(1)}, f32[128,128]{1,0:T(8,128)S(1)}, u32[]{:S(2)}, u32[]{:S(2)}) collective-permute-start(f32[128,128]{1,0:T(8,128)S(1)} %get-tuple-element.15), channel_id=1, source_target_pairs={{0,64},{64,128},{128,192},{192,0},{1,65},{65,129},{129,193},{193,1... | collective-permute-start | bytes 196616 | tf_op jit(solution)/shard_map/ppermute | solution.py:378
  42.6 2.6 %collective-permute-start.9 = (f32[128,128]{1,0:T(8,128)S(1)}, f32[128,128]{1,0:T(8,128)S(1)}, u32[]{:S(2)}, u32[]{:S(2)}) collective-permute-start(f32[128,128]{1,0:T(8,128)S(1)} %get-tuple-element.15), channel_id=1, source_target_pairs={{0,128},{64,192},{128,0},{192,64},{1,129},{65,193},{129,1},{193,65... | collective-permute-start | bytes 196616 | tf_op jit(solution)/shard_map/ppermute | solution.py:378
  45.2 1.1 %collective-permute-start.8 = (f32[128,128]{1,0:T(8,128)S(1)}, f32[128,128]{1,0:T(8,128)S(1)}, u32[]{:S(2)}, u32[]{:S(2)}) collective-permute-start(f32[128,128]{1,0:T(8,128)S(1)} %get-tuple-element.15), channel_id=1, source_target_pairs={{0,192},{64,0},{128,64},{192,128},{1,193},{65,1},{129,65},{193,129... | collective-permute-start | bytes 196616 | tf_op jit(solution)/shard_map/ppermute | solution.py:378
  46.3 0.0 collective-permute-done.10.three_ref
  46.3 1.9 %collective-permute-done.9.two_ref = f32[128,128]{1,0:T(8,128)S(1)} collective-permute-done((f32[128,128]{1,0:T(8,128)S(1)}, f32[128,128]{1,0:T(8,128)S(1)}, u32[]{:S(2)}, u32[]{:S(2)}) %collective-permute-start.9) | collective-permute-done | bytes 65568 | tf_op jit(solution)/shard_map/ppermute | solution.py:378
  48.1 0.5 collective-permute-done.8.one_ref
  48.6 3.6 %smooth.1 = bf16[4,128,4096]{2,1,0:T(8,128)(2,1)} custom-call(f32[128,128]{1,0:T(8,128)S(1)} %collective-permute-done.8.one_ref, f32[128,128]{1,0:T(8,128)S(1)} %collective-permute-done.9.two_ref, f32[128,128]{1,0:T(8,128)S(1)} %collective-permute-done.10.three_ref, f32[384,128]{1,0:T(8,128)S(1)} %get-tuple-element.16.factors_ref, ...), custom_call_target="tpu_custom_call" | custom-call | tf_op jit(solution)/shard_map/smooth/pallas_call | solution.py:338
  (5 shorter events, 0.1 us)
Async XLA Ops:
  2.7 4.3 %collective-permute-start = (f32[136,128]{1,0:T(8,128)S(1)}, f32[136,128]{1,0:T(8,128)S(1)}, u32[]{:S(2)}, u32[]{:S(2)}) collective-permute-start(f32[136,128]{1,0:T(8,128)S(1)} %get-tuple-element.14), channel_id=1, source_target_pairs={{0,1},{1,0},{2,3},{3,2},{4,5},{5,4},{6,7},{7,6},{8,9},{9,8},{10,11... | collective-permute-start | bytes 208904 | tf_op jit(solution)/shard_map/ppermute | solution.py:363
  7.1 3.6 %collective-permute-start.1 = (f32[136,128]{1,0:T(8,128)S(1)}, f32[136,128]{1,0:T(8,128)S(1)}, u32[]{:S(2)}, u32[]{:S(2)}) collective-permute-start(f32[136,128]{1,0:T(8,128)S(1)} %add.21), channel_id=1, source_target_pairs={{0,16},{1,17},{2,18},{3,19},{4,20},{5,21},{6,22},{7,23},{8,24},{9,... | collective-permute-start | bytes 208904 | tf_op jit(solution)/shard_map/ppermute | solution.py:373
  10.7 3.2 %collective-permute-start.2 = (f32[136,128]{1,0:T(8,128)S(1)}, f32[136,128]{1,0:T(8,128)S(1)}, u32[]{:S(2)}, u32[]{:S(2)}) collective-permute-start(f32[136,128]{1,0:T(8,128)S(1)} %add.22), channel_id=1, source_target_pairs={{0,2},{1,3},{2,0},{3,1},{4,6},{5,7},{6,4},{7,5},{8,10},{9,11},{10,... | collective-permute-start | bytes 208904 | tf_op jit(solution)/shard_map/ppermute | solution.py:373
  13.9 7.7 %collective-permute-start.5 = (f32[136,128]{1,0:T(8,128)S(1)}, f32[136,128]{1,0:T(8,128)S(1)}, u32[]{:S(2)}, u32[]{:S(2)}) collective-permute-start(f32[136,128]{1,0:T(8,128)S(1)} %add.23), channel_id=1, source_target_pairs={{0,8},{1,9},{2,10},{3,11},{4,12},{5,13},{6,14},{7,15},{8,0},{9,1},... | collective-permute-start | bytes 208904 | tf_op jit(solution)/shard_map/ppermute | solution.py:373
  19.2 5.9 %collective-permute-start.4 = (f32[136,128]{1,0:T(8,128)S(1)}, f32[136,128]{1,0:T(8,128)S(1)}, u32[]{:S(2)}, u32[]{:S(2)}) collective-permute-start(f32[136,128]{1,0:T(8,128)S(1)} %add.23), channel_id=1, source_target_pairs={{0,12},{1,13},{2,14},{3,15},{4,0},{5,1},{6,2},{7,3},{8,4},{9,5},{1... | collective-permute-start | bytes 208904 | tf_op jit(solution)/shard_map/ppermute | solution.py:373
  19.2 5.9 %collective-permute-start.3 = (f32[136,128]{1,0:T(8,128)S(1)}, f32[136,128]{1,0:T(8,128)S(1)}, u32[]{:S(2)}, u32[]{:S(2)}) collective-permute-start(f32[136,128]{1,0:T(8,128)S(1)} %add.23), channel_id=1, source_target_pairs={{0,4},{1,5},{2,6},{3,7},{4,8},{5,9},{6,10},{7,11},{8,12},{9,13},{1... | collective-permute-start | bytes 208904 | tf_op jit(solution)/shard_map/ppermute | solution.py:373
  25.2 4.8 %collective-permute-start.6 = (f32[136,128]{1,0:T(8,128)S(1)}, f32[136,128]{1,0:T(8,128)S(1)}, u32[]{:S(2)}, u32[]{:S(2)}) collective-permute-start(f32[136,128]{1,0:T(8,128)S(1)} %add_add_fusion), channel_id=1, source_target_pairs={{0,32},{1,33},{2,34},{3,35},{4,36},{5,37},{6,38},{7,39},{8,40},{9,... | collective-permute-start | bytes 208904 | tf_op jit(solution)/shard_map/ppermute | solution.py:373
  35.6 5.3 %collective-permute-start.7 = (f32[256,128]{1,0:T(8,128)S(1)}, f32[256,128]{1,0:T(8,128)S(1)}, u32[]{:S(2)}, u32[]{:S(2)}) collective-permute-start(f32[256,128]{1,0:T(8,128)S(1)} %weights.1.own_ref), channel_id=1, source_target_pairs={{0,1},{1,0},{2,3},{3,2},{4,5},{5,4},{6,7},{7,6},{8,9},{9,8},{10,11... | collective-permute-start | bytes 393224 | tf_op jit(solution)/shard_map/ppermute | solution.py:377
  41.2 5.1 %collective-permute-start.10 = (f32[128,128]{1,0:T(8,128)S(1)}, f32[128,128]{1,0:T(8,128)S(1)}, u32[]{:S(2)}, u32[]{:S(2)}) collective-permute-start(f32[128,128]{1,0:T(8,128)S(1)} %get-tuple-element.15), channel_id=1, source_target_pairs={{0,64},{64,128},{128,192},{192,0},{1,65},{65,129},{129,193},{193,1... | collective-permute-start | bytes 196616 | tf_op jit(solution)/shard_map/ppermute | solution.py:378
  42.6 5.6 %collective-permute-start.9 = (f32[128,128]{1,0:T(8,128)S(1)}, f32[128,128]{1,0:T(8,128)S(1)}, u32[]{:S(2)}, u32[]{:S(2)}) collective-permute-start(f32[128,128]{1,0:T(8,128)S(1)} %get-tuple-element.15), channel_id=1, source_target_pairs={{0,128},{64,192},{128,0},{192,64},{1,129},{65,193},{129,1},{193,65... | collective-permute-start | bytes 196616 | tf_op jit(solution)/shard_map/ppermute | solution.py:378
  45.2 3.4 %collective-permute-start.8 = (f32[128,128]{1,0:T(8,128)S(1)}, f32[128,128]{1,0:T(8,128)S(1)}, u32[]{:S(2)}, u32[]{:S(2)}) collective-permute-start(f32[128,128]{1,0:T(8,128)S(1)} %get-tuple-element.15), channel_id=1, source_target_pairs={{0,192},{64,0},{128,64},{192,128},{1,193},{65,1},{129,65},{193,129... | collective-permute-start | bytes 196616 | tf_op jit(solution)/shard_map/ppermute | solution.py:378

commit v5 on v4

--- a/solution.py
+++ b/solution.py
@@ -302,9 +302,10 @@
 def smooth_kernel(one_ref, two_ref, three_ref, factors_ref, held_ref, out_ref, staged_ref, sems):
     position = lax.axis_index("tm")
     eye = jnp.where(iota((M, M), 0) == iota((M, M), 1), 1.0, 0.0)
-    later = [
-        jnp.where(position + k < 4, ref[...], eye) for k, ref in ((1, one_ref), (2, two_ref), (3, three_ref))
-    ]
+    core = lax.rem(lax.axis_index("space"), 2)
+    one = jnp.where(core == 0, one_ref[...], three_ref[...])
+    three = jnp.where(core == 0, three_ref[...], one_ref[...])
+    later = [jnp.where(position + k < 4, x, eye) for k, x in ((1, one), (2, two_ref[...]), (3, three))]
     suffix = exact_dot(later[0], exact_dot(later[1], later[2])).T
     copies = []
 
@@ -364,10 +365,9 @@
     keep = gram_own(held, index_held, weight_held)
     part = keep + received
     for moves in (
-        [lambda x, z: (x ^ 1, z)],
-        [lambda x, z: (x, z ^ 1)],
-        [lambda x, z: (x, z + 2), lambda x, z: (x, z + 6), lambda x, z: (x, z + 4)],
-        [lambda x, z: (x ^ 2, z)],
+        [lambda x, z: (x ^ 1, z), lambda x, z: (x, z ^ 1), lambda x, z: (x ^ 1, z ^ 1)],
+        [lambda x, z: (x ^ 2, z), lambda x, z: (x, z ^ 2), lambda x, z: (x ^ 2, z ^ 2)],
+        [lambda x, z: (x, z ^ 4)],
     ):
         part = part + sum(
             lax.ppermute(part, "space", [(place(x, z, c), place(*move(x, z), c)) for x, z, c in sites()])
@@ -375,8 +375,15 @@
         )
     own = weights_of(part)
     product, factors = products_of(own, lax.ppermute(own, "space", swap))
-    later = [lax.ppermute(product, "tm", [(g, (g - k) % 4) for g in range(4)]) for k in (3, 2, 1)]
-    later = [later[2], later[1], later[0]]
+    sides = [
+        (g * len(sites()) + place(*s), (g - (1 if s[2] == 0 else 3)) % 4 * len(sites()) + place(*s))
+        for g in range(4)
+        for s in sites()
+    ]
+    second = lax.ppermute(product, "tm", [(g, (g - 2) % 4) for g in range(4)])
+    near = lax.ppermute(product, ("tm", "space"), sides)
+    far = lax.ppermute(near, "space", swap)
+    later = [near, second, far]
     return smooth(later, factors, held)
 
 

time: 53 us -> 52.2 us (0.985)
  waiting for transfers between devices: 15.5 us -> 12.1 us
  starting transfers between devices: 23.3 us -> 25.5 us
    ppermute x6 -> x7, starting transfers between devices: 10.7 us -> 14.6 us  [per_device(): lax.ppermute(part, 'space', [(place(x, z, c), place(*move(x, z), c)) for...]
    ppermute x6 -> x7, waiting for transfers between devices: 12.2 us -> 9.78 us  [per_device(): lax.ppermute(part, 'space', [(place(x, z, c), place(*move(x, z), c)) for...]
    ppermute x1, starting transfers between devices: 4.28 us -> 2.39 us  [per_device(): product, factors = products_of(own, lax.ppermute(own, 'space', swap))]
    ppermute x3, waiting for transfers between devices: 2.34 us -> 1.37 us  [the longest x1 0.62 us: per_device(): second = lax.ppermute(product, 'tm', [(g, (g - 2) % 4) for g in range(4)])]
  transfers between devices with their start and end apart: 11 -> 12, of which waited for: 7 -> 8; matrix products, arithmetic and copies ran while one was open for 0% -> 0% of each run, Pallas kernels for 2% -> 2%
where the time goes in v5:
time: 52.2 us; the launch traced here: 51.2 us
  starting transfers between devices  25.5 us (49%)
  Pallas kernels  13.3 us (25%)
  waiting for transfers between devices  12.1 us (23%)
    ppermute x7, starting transfers between devices, per_device(): lax.ppermute(part, 'space', [(place(x, z, c), place(*move(x, z), c)) for...  14.6 us
    ppermute x7, waiting for transfers between devices, per_device(): lax.ppermute(part, 'space', [(place(x, z, c), place(*move(x, z), c)) for...  9.78 us
    pallas_call x1, Pallas kernels, weights_of(): pl.pallas_call(weights_kernel, out_shape=jax.ShapeDtypeStruct((2 * M, M),...  5.67 us
    pallas_call x1, Pallas kernels, smooth(): pl.pallas_call(smooth_kernel, in_specs=[VMEM] * 5, out_specs=HBM, out_sha...  3.61 us
    ppermute x1, starting transfers between devices, per_device(): received = lax.ppermute(send, 'space', swap)  3.29 us
    pallas_call x1, Pallas kernels, gram_other(): pl.pallas_call(gram_other_kernel, in_specs=[HBM] * 3, out_specs=[VMEM] *...  2.7 us
    ppermute x1, starting transfers between devices, per_device(): second = lax.ppermute(product, 'tm', [(g, (g - 2) % 4) for g in range(4)])  2.63 us
    ppermute x1, starting transfers between devices, per_device(): product, factors = products_of(own, lax.ppermute(own, 'space', swap))  2.39 us
  transfers between devices with their start and end apart: 12, of which 8 were waited for; matrix products, arithmetic and copies ran while one was open for 0% of the time, Pallas kernels for 2%

profile of v5, /device:TPU:1, one launch (start us, length us, event | category | flops | bytes accessed | tf_op | source)
XLA Modules:
  0.0 51.2 jit_solution(2689306795002717240)
XLA Ops:
  0.0 2.7 %gram_other.1 = (f32[136,128]{1,0:T(8,128)S(1)}, bf16[4,128,4096]{2,1,0:T(8,128)(2,1)S(1)}, s32[4,1024]{1,0:T(4,128)S(1)}, f32[4,1024]{1,0:T(4,128)S(1)}) custom-call(bf16[4,128,4096]{2,1,0:T(8,128)(2,1)} %anomalies_ref.1, s32[4,1024]{1,0:T(4,128)} %index_ref.1, f32[4,1024]{1,0:T(4,128)} %weight_ref.1), custom_call_target="tpu_custom_call" | custom-call | flops 268435456 | bytes 2097152 | tf_op jit(solution)/shard_map/gram_other/pallas_call | solution.py:125
  2.7 3.3 %collective-permute-start = (f32[136,128]{1,0:T(8,128)S(1)}, f32[136,128]{1,0:T(8,128)S(1)}, u32[]{:S(2)}, u32[]{:S(2)}) collective-permute-start(f32[136,128]{1,0:T(8,128)S(1)} %get-tuple-element.14), channel_id=1, source_target_pairs={{0,1},{1,0},{2,3},{3,2},{4,5},{5,4},{6,7},{7,6},{8,9},{9,8},{10,11... | collective-permute-start | bytes 208904 | tf_op jit(solution)/shard_map/ppermute | solution.py:364
  6.0 1.0 %gram_own.1 = f32[136,128]{1,0:T(8,128)S(1)} custom-call(bf16[4,128,4096]{2,1,0:T(8,128)(2,1)S(1)} %get-tuple-element.11.held_ref, s32[4,1024]{1,0:T(4,128)S(1)} %get-tuple-element.12.index_ref, f32[4,1024]{1,0:T(4,128)S(1)} %get-tuple-element.13.weight_ref), custom_call_target="tpu_custom_call" | custom-call | flops 268435456 | bytes 2097152 | tf_op jit(solution)/shard_map/gram_own/pallas_call | solution.py:141
  7.0 0.0 collective-permute-done
  7.1 0.9 %collective-permute-start.3 = (f32[136,128]{1,0:T(8,128)S(1)}, f32[136,128]{1,0:T(8,128)S(1)}, u32[]{:S(2)}, u32[]{:S(2)}) collective-permute-start(f32[136,128]{1,0:T(8,128)S(1)} %add.24), channel_id=1, source_target_pairs={{0,18},{1,19},{2,16},{3,17},{4,22},{5,23},{6,20},{7,21},{8,26},{9,... | collective-permute-start | bytes 208904 | tf_op jit(solution)/shard_map/ppermute | solution.py:373
  8.0 0.0 collective-permute-start.2
  8.0 1.8 %collective-permute-start.1 = (f32[136,128]{1,0:T(8,128)S(1)}, f32[136,128]{1,0:T(8,128)S(1)}, u32[]{:S(2)}, u32[]{:S(2)}) collective-permute-start(f32[136,128]{1,0:T(8,128)S(1)} %add.24), channel_id=1, source_target_pairs={{0,16},{1,17},{2,18},{3,19},{4,20},{5,21},{6,22},{7,23},{8,24},{9,... | collective-permute-start | bytes 208904 | tf_op jit(solution)/shard_map/ppermute | solution.py:373
  9.8 1.8 %collective-permute-done.3 = f32[136,128]{1,0:T(8,128)S(1)} collective-permute-done((f32[136,128]{1,0:T(8,128)S(1)}, f32[136,128]{1,0:T(8,128)S(1)}, u32[]{:S(2)}, u32[]{:S(2)}) %collective-permute-start.3) | collective-permute-done | bytes 69664 | tf_op jit(solution)/shard_map/ppermute | solution.py:373
  11.6 0.0 collective-permute-done.2
  11.6 2.0 %collective-permute-done.1 = f32[136,128]{1,0:T(8,128)S(1)} collective-permute-done((f32[136,128]{1,0:T(8,128)S(1)}, f32[136,128]{1,0:T(8,128)S(1)}, u32[]{:S(2)}, u32[]{:S(2)}) %collective-permute-start.1) | collective-permute-done | bytes 69664 | tf_op jit(solution)/shard_map/ppermute | solution.py:373
  13.6 3.0 %collective-permute-start.6 = (f32[136,128]{1,0:T(8,128)S(1)}, f32[136,128]{1,0:T(8,128)S(1)}, u32[]{:S(2)}, u32[]{:S(2)}) collective-permute-start(f32[136,128]{1,0:T(8,128)S(1)} %add_add_fusion.1), channel_id=1, source_target_pairs={{0,36},{1,37},{2,38},{3,39},{4,32},{5,33},{6,34},{7,35},{8,44},{9,... | collective-permute-start | bytes 208904 | tf_op jit(solution)/shard_map/ppermute | solution.py:373
  16.6 0.0 collective-permute-start.5
  16.6 2.1 %collective-permute-start.4 = (f32[136,128]{1,0:T(8,128)S(1)}, f32[136,128]{1,0:T(8,128)S(1)}, u32[]{:S(2)}, u32[]{:S(2)}) collective-permute-start(f32[136,128]{1,0:T(8,128)S(1)} %add_add_fusion.1), channel_id=1, source_target_pairs={{0,32},{1,33},{2,34},{3,35},{4,36},{5,37},{6,38},{7,39},{8,40},{9,... | collective-permute-start | bytes 208904 | tf_op jit(solution)/shard_map/ppermute | solution.py:373
  18.7 4.3 %collective-permute-done.6 = f32[136,128]{1,0:T(8,128)S(1)} collective-permute-done((f32[136,128]{1,0:T(8,128)S(1)}, f32[136,128]{1,0:T(8,128)S(1)}, u32[]{:S(2)}, u32[]{:S(2)}) %collective-permute-start.6) | collective-permute-done | bytes 69664 | tf_op jit(solution)/shard_map/ppermute | solution.py:373
  23.0 0.0 collective-permute-done.5
  23.0 0.0 collective-permute-done.4
  23.1 6.7 %collective-permute-start.7 = (f32[136,128]{1,0:T(8,128)S(1)}, f32[136,128]{1,0:T(8,128)S(1)}, u32[]{:S(2)}, u32[]{:S(2)}) collective-permute-start(f32[136,128]{1,0:T(8,128)S(1)} %add_add_fusion), channel_id=1, source_target_pairs={{0,8},{1,9},{2,10},{3,11},{4,12},{5,13},{6,14},{7,15},{8,0},{9,1},... | collective-permute-start | bytes 208904 | tf_op jit(solution)/shard_map/ppermute | solution.py:373
  29.8 1.7 %collective-permute-done.7 = f32[136,128]{1,0:T(8,128)S(1)} collective-permute-done((f32[136,128]{1,0:T(8,128)S(1)}, f32[136,128]{1,0:T(8,128)S(1)}, u32[]{:S(2)}, u32[]{:S(2)}) %collective-permute-start.7) | collective-permute-done | bytes 69664 | tf_op jit(solution)/shard_map/ppermute | solution.py:373
  31.5 5.7 %weights.1.own_ref = f32[256,128]{1,0:T(8,128)S(1)} custom-call(f32[136,128]{1,0:T(8,128)S(1)} %add.31.total_ref), custom_call_target="tpu_custom_call" | custom-call | tf_op jit(solution)/shard_map/weights/pallas_call | solution.py:272
  37.2 2.4 %collective-permute-start.8 = (f32[256,128]{1,0:T(8,128)S(1)}, f32[256,128]{1,0:T(8,128)S(1)}, u32[]{:S(2)}, u32[]{:S(2)}) collective-permute-start(f32[256,128]{1,0:T(8,128)S(1)} %weights.1.own_ref), channel_id=1, source_target_pairs={{0,1},{1,0},{2,3},{3,2},{4,5},{5,4},{6,7},{7,6},{8,9},{9,8},{10,11... | collective-permute-start | bytes 393224 | tf_op jit(solution)/shard_map/ppermute | solution.py:377
  39.6 1.0 %collective-permute-done.8.other_ref = f32[256,128]{1,0:T(8,128)S(1)} collective-permute-done((f32[256,128]{1,0:T(8,128)S(1)}, f32[256,128]{1,0:T(8,128)S(1)}, u32[]{:S(2)}, u32[]{:S(2)}) %collective-permute-start.8) | collective-permute-done | bytes 131104 | tf_op jit(solution)/shard_map/ppermute | solution.py:377
  40.5 0.3 products.1
  40.8 1.4 %collective-permute-start.9 = (f32[128,128]{1,0:T(8,128)S(1)}, f32[128,128]{1,0:T(8,128)S(1)}, u32[]{:S(2)}, u32[]{:S(2)}) collective-permute-start(f32[128,128]{1,0:T(8,128)S(1)} %get-tuple-element.15), channel_id=1, source_target_pairs={{0,192},{1,65},{2,194},{3,67},{4,196},{5,69},{6,198},{7,71},{8,200... | collective-permute-start | bytes 196616 | tf_op jit(solution)/shard_map/ppermute | solution.py:384
  42.2 2.6 %collective-permute-start.10 = (f32[128,128]{1,0:T(8,128)S(1)}, f32[128,128]{1,0:T(8,128)S(1)}, u32[]{:S(2)}, u32[]{:S(2)}) collective-permute-start(f32[128,128]{1,0:T(8,128)S(1)} %get-tuple-element.15), channel_id=1, source_target_pairs={{0,128},{64,192},{128,0},{192,64},{1,129},{65,193},{129,1},{193,65... | collective-permute-start | bytes 196616 | tf_op jit(solution)/shard_map/ppermute | solution.py:383
  44.8 0.5 collective-permute-done.9.one_ref
  45.3 1.3 %collective-permute-start.11 = (f32[128,128]{1,0:T(8,128)S(1)}, f32[128,128]{1,0:T(8,128)S(1)}, u32[]{:S(2)}, u32[]{:S(2)}) collective-permute-start(f32[128,128]{1,0:T(8,128)S(1)} %collective-permute-done.9.one_ref), channel_id=1, source_target_pairs={{0,1},{1,0},{2,3},{3,2},{4,5},{5,4},{6,7},{7,6},{8,9},{9,8},{10,11... | collective-permute-start | bytes 196616 | tf_op jit(solution)/shard_map/ppermute | solution.py:385
  46.6 0.6 %collective-permute-done.10.two_ref = f32[128,128]{1,0:T(8,128)S(1)} collective-permute-done((f32[128,128]{1,0:T(8,128)S(1)}, f32[128,128]{1,0:T(8,128)S(1)}, u32[]{:S(2)}, u32[]{:S(2)}) %collective-permute-start.10) | collective-permute-done | bytes 65568 | tf_op jit(solution)/shard_map/ppermute | solution.py:383
  47.2 0.3 collective-permute-done.11.three_ref
  47.5 3.6 %smooth.1 = bf16[4,128,4096]{2,1,0:T(8,128)(2,1)} custom-call(f32[128,128]{1,0:T(8,128)S(1)} %collective-permute-done.9.one_ref, f32[128,128]{1,0:T(8,128)S(1)} %collective-permute-done.10.two_ref, f32[128,128]{1,0:T(8,128)S(1)} %collective-permute-done.11.three_ref, f32[384,128]{1,0:T(8,128)S(1)} %get-tuple-element.16.factors_ref, ...), custom_call_target="tpu_custom_call" | custom-call | tf_op jit(solution)/shard_map/smooth/pallas_call | solution.py:339
  (4 shorter events, 0.1 us)
Async XLA Ops:
  2.7 4.3 %collective-permute-start = (f32[136,128]{1,0:T(8,128)S(1)}, f32[136,128]{1,0:T(8,128)S(1)}, u32[]{:S(2)}, u32[]{:S(2)}) collective-permute-start(f32[136,128]{1,0:T(8,128)S(1)} %get-tuple-element.14), channel_id=1, source_target_pairs={{0,1},{1,0},{2,3},{3,2},{4,5},{5,4},{6,7},{7,6},{8,9},{9,8},{10,11... | collective-permute-start | bytes 208904 | tf_op jit(solution)/shard_map/ppermute | solution.py:364
  7.1 4.5 %collective-permute-start.3 = (f32[136,128]{1,0:T(8,128)S(1)}, f32[136,128]{1,0:T(8,128)S(1)}, u32[]{:S(2)}, u32[]{:S(2)}) collective-permute-start(f32[136,128]{1,0:T(8,128)S(1)} %add.24), channel_id=1, source_target_pairs={{0,18},{1,19},{2,16},{3,17},{4,22},{5,23},{6,20},{7,21},{8,26},{9,... | collective-permute-start | bytes 208904 | tf_op jit(solution)/shard_map/ppermute | solution.py:373
  8.0 3.6 %collective-permute-start.2 = (f32[136,128]{1,0:T(8,128)S(1)}, f32[136,128]{1,0:T(8,128)S(1)}, u32[]{:S(2)}, u32[]{:S(2)}) collective-permute-start(f32[136,128]{1,0:T(8,128)S(1)} %add.24), channel_id=1, source_target_pairs={{0,2},{1,3},{2,0},{3,1},{4,6},{5,7},{6,4},{7,5},{8,10},{9,11},{10,... | collective-permute-start | bytes 208904 | tf_op jit(solution)/shard_map/ppermute | solution.py:373
  8.0 5.5 %collective-permute-start.1 = (f32[136,128]{1,0:T(8,128)S(1)}, f32[136,128]{1,0:T(8,128)S(1)}, u32[]{:S(2)}, u32[]{:S(2)}) collective-permute-start(f32[136,128]{1,0:T(8,128)S(1)} %add.24), channel_id=1, source_target_pairs={{0,16},{1,17},{2,18},{3,19},{4,20},{5,21},{6,22},{7,23},{8,24},{9,... | collective-permute-start | bytes 208904 | tf_op jit(solution)/shard_map/ppermute | solution.py:373
  13.6 9.5 %collective-permute-start.6 = (f32[136,128]{1,0:T(8,128)S(1)}, f32[136,128]{1,0:T(8,128)S(1)}, u32[]{:S(2)}, u32[]{:S(2)}) collective-permute-start(f32[136,128]{1,0:T(8,128)S(1)} %add_add_fusion.1), channel_id=1, source_target_pairs={{0,36},{1,37},{2,38},{3,39},{4,32},{5,33},{6,34},{7,35},{8,44},{9,... | collective-permute-start | bytes 208904 | tf_op jit(solution)/shard_map/ppermute | solution.py:373
  16.6 6.5 %collective-permute-start.5 = (f32[136,128]{1,0:T(8,128)S(1)}, f32[136,128]{1,0:T(8,128)S(1)}, u32[]{:S(2)}, u32[]{:S(2)}) collective-permute-start(f32[136,128]{1,0:T(8,128)S(1)} %add_add_fusion.1), channel_id=1, source_target_pairs={{0,4},{1,5},{2,6},{3,7},{4,0},{5,1},{6,2},{7,3},{8,12},{9,13},{10,... | collective-permute-start | bytes 208904 | tf_op jit(solution)/shard_map/ppermute | solution.py:373
  16.6 6.5 %collective-permute-start.4 = (f32[136,128]{1,0:T(8,128)S(1)}, f32[136,128]{1,0:T(8,128)S(1)}, u32[]{:S(2)}, u32[]{:S(2)}) collective-permute-start(f32[136,128]{1,0:T(8,128)S(1)} %add_add_fusion.1), channel_id=1, source_target_pairs={{0,32},{1,33},{2,34},{3,35},{4,36},{5,37},{6,38},{7,39},{8,40},{9,... | collective-permute-start | bytes 208904 | tf_op jit(solution)/shard_map/ppermute | solution.py:373
  23.1 8.4 %collective-permute-start.7 = (f32[136,128]{1,0:T(8,128)S(1)}, f32[136,128]{1,0:T(8,128)S(1)}, u32[]{:S(2)}, u32[]{:S(2)}) collective-permute-start(f32[136,128]{1,0:T(8,128)S(1)} %add_add_fusion), channel_id=1, source_target_pairs={{0,8},{1,9},{2,10},{3,11},{4,12},{5,13},{6,14},{7,15},{8,0},{9,1},... | collective-permute-start | bytes 208904 | tf_op jit(solution)/shard_map/ppermute | solution.py:373
  37.2 3.4 %collective-permute-start.8 = (f32[256,128]{1,0:T(8,128)S(1)}, f32[256,128]{1,0:T(8,128)S(1)}, u32[]{:S(2)}, u32[]{:S(2)}) collective-permute-start(f32[256,128]{1,0:T(8,128)S(1)} %weights.1.own_ref), channel_id=1, source_target_pairs={{0,1},{1,0},{2,3},{3,2},{4,5},{5,4},{6,7},{7,6},{8,9},{9,8},{10,11... | collective-permute-start | bytes 393224 | tf_op jit(solution)/shard_map/ppermute | solution.py:377
  40.8 4.5 %collective-permute-start.9 = (f32[128,128]{1,0:T(8,128)S(1)}, f32[128,128]{1,0:T(8,128)S(1)}, u32[]{:S(2)}, u32[]{:S(2)}) collective-permute-start(f32[128,128]{1,0:T(8,128)S(1)} %get-tuple-element.15), channel_id=1, source_target_pairs={{0,192},{1,65},{2,194},{3,67},{4,196},{5,69},{6,198},{7,71},{8,200... | collective-permute-start | bytes 196616 | tf_op jit(solution)/shard_map/ppermute | solution.py:384
  42.2 5.0 %collective-permute-start.10 = (f32[128,128]{1,0:T(8,128)S(1)}, f32[128,128]{1,0:T(8,128)S(1)}, u32[]{:S(2)}, u32[]{:S(2)}) collective-permute-start(f32[128,128]{1,0:T(8,128)S(1)} %get-tuple-element.15), channel_id=1, source_target_pairs={{0,128},{64,192},{128,0},{192,64},{1,129},{65,193},{129,1},{193,65... | collective-permute-start | bytes 196616 | tf_op jit(solution)/shard_map/ppermute | solution.py:383
  45.3 2.2 %collective-permute-start.11 = (f32[128,128]{1,0:T(8,128)S(1)}, f32[128,128]{1,0:T(8,128)S(1)}, u32[]{:S(2)}, u32[]{:S(2)}) collective-permute-start(f32[128,128]{1,0:T(8,128)S(1)} %collective-permute-done.9.one_ref), channel_id=1, source_target_pairs={{0,1},{1,0},{2,3},{3,2},{4,5},{5,4},{6,7},{7,6},{8,9},{9,8},{10,11... | collective-permute-start | bytes 196616 | tf_op jit(solution)/shard_map/ppermute | solution.py:385
